TPU v7x, 512 devices: a whole 4x8x8 slice. The times are simulated.
512 devices in a mesh: ctx: 32 (over x_hi, y, core), batch: 16 (over z, x_lo).
Axes of the slice: x: 4 (x_hi: 2, x_lo: 2; x = x_hi * 2 + x_lo), y: 8, z: 8, core: 2. Of those that a mesh axis runs over, the one named last changes fastest.
Arguments:
- seq_in: bfloat16 [16, 4096, 512], P('batch', 'ctx'), may hold values from -6 to 6
- w_in: bfloat16 [512, 2048], replicated, may hold values from -0.25 to 0.25
- w_out: bfloat16 [512, 512], replicated, may hold values from -0.25 to 0.25
- pos_emb: bfloat16 [16, 4096, 512], P('batch', 'ctx'), may hold values from -0.29882812 to 0.29882812
- pos_ids: int32 [16, 4096], P('batch', 'ctx'), may hold values from 0 to 3999999, as said below
- neg_emb: bfloat16 [128, 512], P('batch'), may hold values from -0.29882812 to 0.29882812
- neg_ids: int32 [128], P('batch'), may hold values from 0 to 3999999
- neg_counts: int32 [128], P('batch'), may hold values from 1000 to 99999
Outputs:
- loss: float32 [16, 4096], P('batch', 'ctx')
- d_seq: bfloat16 [16, 4096, 512], P('batch', 'ctx')
- d_neg: float32 [128, 512], P('batch')
Inputs may be any that keep to these rules, and one draw needn't show every extreme that they name: `pos_ids`: item ids; many positions name the item of one of the sampled negatives.
All inputs are finite; a program needn't handle non-finite values.
Results may differ from a plain program's by a relative error of at most 0.008.
Values may be sent and summed in bfloat16 or wider, within the bound.
A program may use at most 128 MiB of HBM per device.

v0:
```python
import math

import jax
import jax.numpy as jnp
from jax import lax
from jax.sharding import PartitionSpec as P

HEADS = 8
HEAD = 64
D = 512


SOFTMAX_TEMPER = 0.05


def silu_slope(scores):
    sigma = jax.nn.sigmoid(scores)
    return sigma * (1.0 + scores * (1.0 - sigma))


def split_heads(matrix):
    return matrix.reshape(matrix.shape[0], HEADS, HEAD)


def shards(seq_in, w_in, w_out, pos_emb, pos_ids, neg_emb, neg_ids, neg_counts):
    tokens = seq_in.shape[1]
    score_scale = HEAD ** (-0.5)
    offset = lax.axis_index("ctx") * tokens
    row_pos = offset + lax.iota(jnp.int32, tokens)
    neg_float = neg_emb.astype(jnp.float32)
    neg_scale = lax.rsqrt(jnp.sum(neg_float * neg_float, axis=1, keepdims=True) + 1e-06)
    neg_unit = neg_float * neg_scale
    every_unit_vector, all_ids, all_counts = (
        lax.all_gather(neg_unit.astype(jnp.bfloat16), "batch", axis=0, tiled=True),
        lax.all_gather(neg_ids, "batch", axis=0, tiled=True),
        lax.all_gather(neg_counts, "batch", axis=0, tiled=True),
    )
    count_float = all_counts.astype(jnp.float32)
    log_sample_share = jnp.log(all_counts.shape[0] * count_float / jnp.sum(count_float))
    seq_x = seq_in[0]
    pre_act = jnp.dot(seq_x, w_in, preferred_element_type=jnp.float32)
    proj = jax.nn.silu(pre_act).astype(jnp.bfloat16)
    gate_u = proj[:, :D].astype(jnp.float32)
    value_rows = proj[:, D : 2 * D]
    query_rows = proj[:, 2 * D : 3 * D]
    key_rows = proj[:, 3 * D :]
    all_values, all_keys = (
        lax.all_gather(value_rows, "ctx", axis=0, tiled=True),
        lax.all_gather(key_rows, "ctx", axis=0, tiled=True),
    )
    length = all_keys.shape[0]
    block_rows = math.gcd(length, 512)
    heads_keys = split_heads(all_keys)
    heads_values = split_heads(all_values)
    local_q = split_heads(query_rows)
    local_k = split_heads(key_rows)
    local_v = split_heads(value_rows)
    empty = jnp.zeros((tokens, HEADS, HEAD), jnp.float32)

    def forward_step(index, carry):
        start = index * block_rows
        keys_blk = lax.dynamic_slice_in_dim(heads_keys, start, block_rows, 0)
        values_blk = lax.dynamic_slice_in_dim(heads_values, start, block_rows, 0)
        scores = (
            jnp.einsum("ihe,jhe->hij", local_q, keys_blk, preferred_element_type=jnp.float32)
            * score_scale
        )
        allowed = ((start + lax.iota(jnp.int32, block_rows))[None, :] <= row_pos[:, None])[None]
        weights = jnp.where(allowed, jax.nn.silu(scores), 0.0).astype(jnp.bfloat16)
        return carry + jnp.einsum(
            "hij,jhe->ihe", weights, values_blk, preferred_element_type=jnp.float32
        )

    mixed = lax.fori_loop(0, length // block_rows, forward_step, empty).reshape(tokens, D)
    centred = mixed - jnp.mean(mixed, axis=1, keepdims=True)
    inv_std = lax.rsqrt(jnp.mean(centred * centred, axis=1, keepdims=True) + 1e-05)
    normed = centred * inv_std
    gated = (normed * gate_u).astype(jnp.bfloat16)
    outputs = seq_x.astype(jnp.float32) + jnp.dot(gated, w_out, preferred_element_type=jnp.float32)
    out_scale = lax.rsqrt(jnp.sum(outputs * outputs, axis=1, keepdims=True) + 1e-06)
    user_vector = outputs * out_scale
    user_rounded = user_vector.astype(jnp.bfloat16)
    pos_float = pos_emb[0].astype(jnp.float32)
    positive_unit = pos_float * lax.rsqrt(
        jnp.sum(pos_float * pos_float, axis=1, keepdims=True) + 1e-06
    )
    positive_item = jnp.sum(user_vector * positive_unit, axis=1) / SOFTMAX_TEMPER
    score_logits = (
        jnp.einsum("id,nd->in", user_rounded, every_unit_vector, preferred_element_type=jnp.float32)
        / SOFTMAX_TEMPER
        - log_sample_share[None, :]
    )
    allowed_items = pos_ids[0][:, None] != all_ids[None, :]
    terms = jnp.where(allowed_items, jnp.exp(score_logits), 0.0)
    pos_exp = jnp.exp(positive_item)
    denom = pos_exp + jnp.sum(terms, axis=1)
    loss = jnp.log(denom) - positive_item
    positive_gradient = pos_exp / denom - 1.0
    probabilities = (terms / denom[:, None]).astype(jnp.bfloat16)
    user_gradient = (
        positive_gradient[:, None] * positive_unit / SOFTMAX_TEMPER
        + jnp.dot(probabilities, every_unit_vector, preferred_element_type=jnp.float32)
        / SOFTMAX_TEMPER
    )
    unit_gradient = (
        jnp.einsum("wz,wb->zb", probabilities, user_rounded, preferred_element_type=jnp.float32)
        / SOFTMAX_TEMPER
    )
    owned = lax.psum_scatter(
        unit_gradient.astype(jnp.bfloat16), "batch", scatter_dimension=0, tiled=True
    ).astype(jnp.float32)
    d_total = lax.psum(owned, "ctx")
    d_neg = neg_scale * (d_total - neg_unit * jnp.sum(neg_unit * d_total, axis=1, keepdims=True))
    d_outputs = out_scale * (
        user_gradient - user_vector * jnp.sum(user_vector * user_gradient, axis=1, keepdims=True)
    )
    d_gated = jnp.einsum(
        "ik,dk->id", d_outputs.astype(jnp.bfloat16), w_out, preferred_element_type=jnp.float32
    )
    d_normed = d_gated * gate_u
    d_gate = d_gated * normed
    d_mixed = inv_std * (
        d_normed
        - jnp.mean(d_normed, axis=1, keepdims=True)
        - normed * jnp.mean(d_normed * normed, axis=1, keepdims=True)
    )
    d_rows = d_mixed.astype(jnp.bfloat16)
    d_heads = split_heads(d_rows)

    def query_step(index, carry):
        start = index * block_rows
        keys_blk = lax.dynamic_slice_in_dim(heads_keys, start, block_rows, 0)
        values_blk = lax.dynamic_slice_in_dim(heads_values, start, block_rows, 0)
        scores = (
            jnp.einsum("ihe,jhe->hij", local_q, keys_blk, preferred_element_type=jnp.float32)
            * score_scale
        )
        allowed = ((start + lax.iota(jnp.int32, block_rows))[None, :] <= row_pos[:, None])[None]
        d_weights = jnp.einsum(
            "ihe,jhe->hij", d_heads, values_blk, preferred_element_type=jnp.float32
        )
        d_scores = jnp.where(allowed, d_weights * silu_slope(scores) * score_scale, 0.0).astype(
            jnp.bfloat16
        )
        return carry + jnp.einsum(
            "hij,jhe->ihe", d_scores, keys_blk, preferred_element_type=jnp.float32
        )

    d_queries = lax.fori_loop(0, length // block_rows, query_step, empty)
    queries_piece = lax.all_gather(query_rows, "ctx", axis=0, tiled=True)
    grads_piece = lax.all_gather(d_rows, "ctx", axis=0, tiled=True)
    count = queries_piece.shape[0]
    inner = math.gcd(count, 512)

    def inner_step(index, sums):
        first = index * inner
        query_blk = split_heads(lax.dynamic_slice_in_dim(queries_piece, first, inner, 0))
        grad_blk = split_heads(lax.dynamic_slice_in_dim(grads_piece, first, inner, 0))
        query_pos = first + lax.iota(jnp.int32, inner)
        scores = (
            jnp.einsum("ihe,jhe->hij", query_blk, local_k, preferred_element_type=jnp.float32)
            * score_scale
        )
        allowed = (row_pos[None, :] <= query_pos[:, None])[None]
        weights = jnp.where(allowed, jax.nn.silu(scores), 0.0).astype(jnp.bfloat16)
        d_weights = jnp.einsum(
            "ihe,jhe->hij", grad_blk, local_v, preferred_element_type=jnp.float32
        )
        d_scores = jnp.where(allowed, d_weights * silu_slope(scores) * score_scale, 0.0).astype(
            jnp.bfloat16
        )
        new_keys = sums[0] + jnp.einsum(
            "hij,ihe->jhe", d_scores, query_blk, preferred_element_type=jnp.float32
        )
        new_values = sums[1] + jnp.einsum(
            "hij,ihe->jhe", weights, grad_blk, preferred_element_type=jnp.float32
        )
        return (new_keys, new_values)

    d_keys, d_values = lax.fori_loop(0, count // inner, inner_step, (empty, empty))
    d_proj = jnp.concatenate(
        [
            d_gate,
            d_values.reshape(tokens, D),
            d_queries.reshape(tokens, D),
            d_keys.reshape(tokens, D),
        ],
        axis=1,
    )
    d_pre = (d_proj * silu_slope(pre_act)).astype(jnp.bfloat16)
    d_seq = (
        d_outputs + jnp.einsum("ik,dk->id", d_pre, w_in, preferred_element_type=jnp.float32)
    ).astype(jnp.bfloat16)
    return (loss[None], d_seq[None], d_neg)


def solution(mesh):
    in_specs = (
        P("batch", "ctx", None),
        P(),
        P(),
        P("batch", "ctx", None),
        P("batch", "ctx"),
        P("batch", None),
        P("batch"),
        P("batch"),
    )
    out_specs = (P("batch", "ctx"), P("batch", "ctx", None), P("batch", None))
    return jax.shard_map(shards, mesh=mesh, in_specs=in_specs, out_specs=out_specs, check_vma=False)
```

profile of v0, /device:TPU:1, one launch (start us, length us, event | category | flops | bytes accessed | tf_op | source)
XLA Modules:
  0.0 607.7 jit_solution(220923983265694282)
XLA Ops:
  15.3 19.5 %all-reduce.2 = (s32[128]{0:T(128)S(1)}, s32[128]{0:T(128)}) all-reduce(s32[128]{0:T(128)S(1)} %dynamic-update-slice.1, s32[128]{0:T(128)S(1)} %dynamic-update-slice), channel_id=1, replica_groups=mesh['ctx'=32,'batch'=16] {'batch'}, use_global_device_ids=true, to_apply=%add.1 | all-reduce | flops 256 | bytes 2048
  35.0 26.8 %all_gather.24 = bf16[128,512]{1,0:T(8,128)(2,1)} all-gather(bf16[8,512]{1,0:T(8,128)(2,1)S(1)} %fusion.98), channel_id=1, replica_groups=mesh['ctx'=32,'batch'=16] {'batch'}, dimensions={0}, use_global_device_ids=true | all-gather | bytes 139264 | tf_op jit(solution)/shard_map/all_gather | solution.py:34
  64.2 45.5 %all-gather.5.cloned.1.call-done = bf16[4096,512]{1,0:T(8,128)(2,1)} async-done(((bf16[128,512]{1,0:T(8,128)(2,1)}), bf16[4096,512]{1,0:T(8,128)(2,1)}) %all-gather.5.cloned.1.call-update) | async-done | bytes 4194320 | tf_op jit(solution)/shard_map/all_gather | solution.py:48
  109.7 6.4 %copy.27 = bf16[4096,512]{0,1:T(8,128)(2,1)} copy(bf16[4096,512]{1,0:T(8,128)(2,1)} %all-gather.5.cloned.1.call-done) | data formatting | bytes 8388608 | tf_op jit(solution)/shard_map/all_gather | solution.py:48
  116.1 86.6 %all-gather.7.cloned.1.call-done = bf16[4096,512]{1,0:T(8,128)(2,1)} async-done(((bf16[128,512]{1,0:T(8,128)(2,1)}), bf16[4096,512]{1,0:T(8,128)(2,1)}) %all-gather.7.cloned.1.call-update) | async-done | bytes 4194320 | tf_op jit(solution)/shard_map/all_gather | solution.py:49
  202.7 6.4 %copy.28 = bf16[4096,512]{0,1:T(8,128)(2,1)} copy(bf16[4096,512]{1,0:T(8,128)(2,1)} %all-gather.7.cloned.1.call-done) | data formatting | bytes 8388608 | tf_op jit(solution)/shard_map/all_gather | solution.py:49
  209.1 19.7 %while.44 = (s32[]{:T(128)}, f32[128,8,64]{0,2,1:T(8,128)S(1)}, bf16[4096,8,64]{0,2,1:T(8,128)(2,1)}, bf16[4096,8,64]{0,2,1:T(8,128)(2,1)}, bf16[128,8,64]{0,2,1...) while((s32[]{:T(128)}, f32[128,8,64]{0,2,1:T(8,128)S(1)}, ...), condition=%wide.region_1.0_spmd.clone, body=%wide.region_0.0_spmd.clone.sunk | while | flops 138084992 | bytes 1841828 | solution.py:74
  245.2 57.4 %while.46 = (s32[]{:T(128)}, f32[128,8,64]{0,2,1:T(8,128)}, bf16[4096,8,64]{0,2,1:T(8,128)(2,1)}, bf16[4096,8,64]{0,2,1:T(8,128)(2,1)}, bf16[128,8,64]{2,1,0:T(8...) while((s32[]{:T(128)}, f32[128,8,64]{0,2,1:T(8,128)}, ...), condition=%wide.region_16.17_spmd.clone, body=%wide.region_15.16_spmd.clone.sunk | while | flops 207815296 | bytes 9313028 | solution.py:149
  255.5 3.3 fusion.162
  262.6 3.4 fusion.162
  269.8 3.4 fusion.162
  277.0 3.4 fusion.162
  291.3 3.3 fusion.162
  304.9 125.1 %psum.7 = f32[8,512]{1,0:T(8,128)S(1)} all-reduce(bf16[8,512]{1,0:T(8,128)(2,1)} %reduce-scatter.2.cloned.1.call-done), channel_id=1, replica_groups=mesh['ctx'=32,'batch'=16] {'ctx'}, use_global_device_ids=true, to_apply=%region_18.19 | all-reduce | flops 4096 | bytes 24576 | tf_op jit(solution)/shard_map/psum | solution.py:112
  430.8 61.0 %all-gather.11.cloned.1.call-done = bf16[4096,512]{1,0:T(8,128)(2,1)} async-done(((bf16[128,512]{1,0:T(8,128)(2,1)}), bf16[4096,512]{1,0:T(8,128)(2,1)}) %all-gather.11.cloned.1.call-update) | async-done | bytes 4194320 | tf_op jit(solution)/shard_map/all_gather | solution.py:151
  491.8 104.2 %while.45 = (s32[]{:T(128)}, f32[128,8,64]{0,2,1:T(8,128)}, f32[128,8,64]{0,2,1:T(8,128)}, bf16[4096,512]{1,0:T(8,128)(2,1)}, bf16[4096,512]{1,0:T(8,128)(2,1)},...) while((s32[]{:T(128)}, f32[128,8,64]{0,2,1:T(8,128)}, ...), condition=%wide.region_14.15_spmd.clone, body=%wide.region_13.14_spmd.clone.sunk | while | flops 278725248 | bytes 16192726 | solution.py:180
  501.2 3.6 fusion.154
  514.1 3.7 fusion.154
  527.1 3.7 fusion.154
  540.2 3.7 fusion.154
  553.2 3.7 fusion.154
  566.3 3.7 fusion.154
  579.3 3.7 fusion.154
  592.3 3.7 fusion.154
  (303 shorter events, 168.3 us)
Async XLA Ops:
  7.2 7.6 %copy-start.27 = (s32[8]{0:T(128)S(1)}, s32[8]{0:T(128)}, u32[]{:S(2)}) copy-start(s32[8]{0:T(128)} %param.20) | copy-start | bytes 100
  7.2 7.9 %copy-start.28 = (s32[8]{0:T(128)S(1)}, s32[8]{0:T(128)}, u32[]{:S(2)}) copy-start(s32[8]{0:T(128)} %param.21) | copy-start | bytes 100
  7.2 27.6 %copy-start.15 = (bf16[8,512]{1,0:T(8,128)(2,1)S(1)}, bf16[8,512]{1,0:T(8,128)(2,1)}, u32[]{:S(2)}) copy-start(bf16[8,512]{1,0:T(8,128)(2,1)} %param.19) | copy-start | bytes 24580
  7.2 55.1 %copy-start.3 = (bf16[1,128,512]{2,1,0:T(8,128)(2,1)S(1)}, bf16[1,128,512]{2,1,0:T(8,128)(2,1)}, u32[]{:S(2)}) copy-start(bf16[1,128,512]{2,1,0:T(8,128)(2,1)} %param.17) | copy-start | bytes 393220
  7.2 102.5 %all-gather.5.cloned.1.call-start = ((), (), s32[]{:S(2)}) async-start(), calls=%async_computation.1 | async-start | bytes 4325376 | tf_op jit(solution)/shard_map/all_gather | solution.py:48
  11.9 104.2 %copy-start.5 = (bf16[128,512]{1,0:T(8,128)(2,1)}, bf16[128,512]{1,0:T(8,128)(2,1)S(1)}, u32[]{:S(2)}) copy-start(bf16[128,512]{1,0:T(8,128)(2,1)S(1)} %get-tuple-element.547) | copy-start | bytes 393220
  11.9 190.8 %all-gather.7.cloned.1.call-start = ((), (), s32[]{:S(2)}) async-start(), calls=%async_computation.2 | async-start | bytes 4325376 | tf_op jit(solution)/shard_map/all_gather | solution.py:49
  12.7 292.2 %reduce-scatter.2.cloned.1.call-start = ((), (), s32[]{:S(2)}) async-start(), calls=%async_computation.5 | async-start | bytes 139264 | tf_op jit(solution)/shard_map/reduce_scatter | solution.py:109
  34.9 81.2 %copy-start.19 = (f32[8]{0:T(128)}, f32[8]{0:T(128)S(1)}, u32[]{:S(2)}) copy-start(f32[8]{0:T(128)S(1)} %add_rsqrt_fusion) | copy-start | bytes 100
  209.1 20.5 %copy-start.2 = (bf16[512,512]{1,0:T(8,128)(2,1)S(1)}, bf16[512,512]{1,0:T(8,128)(2,1)}, u32[]{:S(2)}) copy-start(bf16[512,512]{1,0:T(8,128)(2,1)} %param.16) | copy-start | bytes 1572868
  229.6 10.5 %copy-start.4 = (bf16[1,128,512]{2,1,0:T(8,128)(2,1)S(1)}, bf16[1,128,512]{2,1,0:T(8,128)(2,1)}, u32[]{:S(2)}) copy-start(bf16[1,128,512]{2,1,0:T(8,128)(2,1)} %param.17) | copy-start | bytes 393220
  229.6 10.5 %copy-start.7 = (bf16[128,512]{1,0:T(8,128)(2,1)S(1)}, bf16[128,512]{1,0:T(8,128)(2,1)}, u32[]{:S(2)}) copy-start(bf16[128,512]{1,0:T(8,128)(2,1)} %all_gather.24) | copy-start | bytes 393220
  235.0 195.9 %all-gather.9.cloned.1.call-start = ((), (), s32[]{:S(2)}) async-start(), calls=%async_computation.3 | async-start | bytes 4325376 | tf_op jit(solution)/shard_map/all_gather | solution.py:150
  235.5 256.3 %all-gather.11.cloned.1.call-start = ((), (), s32[]{:S(2)}) async-start(), calls=%async_computation.4 | async-start | bytes 4325376 | tf_op jit(solution)/shard_map/all_gather | solution.py:151
  241.2 3.2 copy-start.9
  241.3 3.2 copy-start.21
  245.1 59.2 %copy-start.24 = (f32[128]{0:T(128)S(1)}, f32[128]{0:T(128)}, u32[]{:S(2)}) copy-start(f32[128]{0:T(128)} %copy-done.23) | copy-start | bytes 1540
  245.2 59.2 %copy-start.26 = (f32[128]{0:T(128)S(1)}, f32[128]{0:T(128)}, u32[]{:S(2)}) copy-start(f32[128]{0:T(128)} %copy-done.25) | copy-start | bytes 1540
  245.2 184.8 %copy-start.20 = (f32[8]{0:T(128)S(1)}, f32[8]{0:T(128)}, u32[]{:S(2)}) copy-start(f32[8]{0:T(128)} %copy-done.19) | copy-start | bytes 100
  491.8 106.4 %copy-start.22 = (f32[128]{0:T(128)S(1)}, f32[128]{0:T(128)}, u32[]{:S(2)}) copy-start(f32[128]{0:T(128)} %copy-done.21) | copy-start | bytes 1540
  524.0 3.2 copy-start.1
  537.0 3.2 copy-start.1
  550.1 3.2 copy-start.1
  576.1 3.2 copy-start.1
  (38 other events, 80.3 us)
Sparse Core Ops, SparseCore 0:
  12.0 97.6 all-gather.4
  113.7 88.9 all-gather.6
  235.1 58.7 reduce-scatter.1
  297.1 101.8 all-gather.8
  402.8 88.9 all-gather.10
where the time goes:
time: 610 us; the launch traced here: 608 us
  waiting for transfers between devices  194 us (32%)
  blocking collectives  171 us (28%)
  matrix products  158 us (26%)
  local copies, waits for them, and re-layouts  52.5 us (9%)
  other arithmetic  15.9 us (3%)
  between operations  14.8 us (2%)
    psum x1, blocking collectives, shards(): d_total = lax.psum(owned, 'ctx')  125 us
    all_gather x1, waiting for transfers between devices, shards(): lax.all_gather(key_rows, 'ctx', axis=0, tiled=True)  86.6 us
    all_gather x1, waiting for transfers between devices, shards(): grads_piece = lax.all_gather(d_rows, 'ctx', axis=0, tiled=True)  61 us
    all_gather x1, waiting for transfers between devices, shards(): lax.all_gather(value_rows, 'ctx', axis=0, tiled=True)  45.5 us
    dot_general x8, matrix products, inner_step(): jnp.einsum('hij,ihe->jhe', d_scores, query_blk, preferred_element_type=jn...  29.6 us
    dot_general x8, matrix products, query_step(): jnp.einsum('hij,jhe->ihe', d_scores, keys_blk, preferred_element_type=jnp...  26.8 us
    all_gather x1, blocking collectives, shards(): lax.all_gather(neg_unit.astype(jnp.bfloat16), 'batch', axis=0, tiled=True)  26.8 us
    dot_general x8, matrix products, inner_step(): jnp.einsum('hij,ihe->jhe', weights, grad_blk, preferred_element_type=jnp....  25.2 us
  transfers between devices with their start and end apart: 5, of which 3 were waited for; matrix products, arithmetic and copies ran while one was open for 12% of the time, Pallas kernels for 0%

commit v1 on v0

v1 whole, which is shorter than its diff:
```python
import jax
import jax.numpy as jnp
from jax import lax
from jax.experimental import pallas as pl
from jax.experimental.pallas import tpu as pltpu
from jax.sharding import PartitionSpec as P

MESH = pl.DeviceIdType.MESH
F32, BF16, I32 = jnp.float32, jnp.bfloat16, jnp.int32
HEAD = 64
ROWS = 128
TEMPER_INV = 20.0


def dot_nn(a, b):
    return lax.dot_general(a, b, (((1,), (0,)), ((), ())), preferred_element_type=F32)


def dot_nt(a, b):
    return lax.dot_general(a, b, (((1,), (1,)), ((), ())), preferred_element_type=F32)


def swap(v):
    return pltpu.roll(v, 64, 1)


def low(shape):
    return lax.broadcasted_iota(I32, shape, 1) < HEAD


def slope(v):
    g = jax.nn.sigmoid(v)
    return g * (1.0 + v * (1.0 - g))


def pack_rows(tile, which):
    top, bottom = tile[:64], tile[64:]
    if which == 0:
        return jnp.where(low(top.shape), top, swap(bottom))
    return jnp.where(low(top.shape), swap(top), bottom)


def unpack_pair(even, odd):
    top = jnp.where(low(even.shape), even, swap(odd))
    bottom = jnp.where(low(even.shape), swap(even), odd)
    return jnp.concatenate([top, bottom], axis=0)


def kernel(
    NY, NB,
    seq_ref, w_in_ref, w_out_ref, pos_ref, pid_ref, neg_ref, nid_ref, ncnt_ref,
    loss_ref, dseq_ref, dneg_ref,
    pre, skv, sq, kv, rq, qz, acc, smix, rmix, sdm, rdm, dmz, qdt, dq, dkv,
    sibo, sibx, sx, rx, sret, rret, sretq, rretq, dout, dpre, negs, nega, gsend, grecv, g1, g2, g3, g4, gfin,
    kv_s, kv_r, q_s, q_r, rel_s, rel_r, xf_s, xf_r, xr_s, xr_r, mix_s, mix_r, dm_s, dm_r,
    so_s, so_r, sx_s, sx_r, xx_s, xx_r, ret_s, ret_r, retq_s, retq_r,
    neg_s, neg_r, gb_s, gb_r, g1_s, g1_r, gc_s, gc_r, g4_s, g4_r,
):
    D = HEAD * NY
    T = NY // 2
    me = lax.axis_index("ctx")
    b = lax.axis_index("batch")
    c = lax.rem(me, 2)
    y = lax.rem(lax.div(me, 2), NY)
    x = lax.div(me, 2 * NY)

    def at(xx, yy, cc):
        return (xx * NY + yy) * 2 + cc

    def yo(d):
        return lax.rem(y + d, NY)

    def bo(d):
        return lax.rem(b + d, NB)

    sib = at(x, y, 1 - c)
    others = [at(x, yo(d), c) for d in range(1, NY)]
    across = [at(1 - x, yo(d), c) for d in range(NY)]

    def copy(src, dst, ss, rs, ctx=None, batch=None):
        where = {"ctx": ctx} if batch is None else {"batch": batch}
        return pltpu.make_async_remote_copy(
            src_ref=src, dst_ref=dst, send_sem=ss, recv_sem=rs, device_id=where, device_id_type=MESH
        )

    barrier = pltpu.get_barrier_semaphore()
    for p in [sib] + others + across:
        pl.semaphore_signal(barrier, inc=1, device_id={"ctx": p}, device_id_type=MESH)
    for d in range(1, NB):
        pl.semaphore_signal(barrier, inc=1, device_id={"batch": bo(d)}, device_id_type=MESH)

    xin = seq_ref[0]
    lane = lax.broadcasted_iota(I32, (ROWS, 128), 1)
    lo = lane < HEAD

    for j in range(NY // 2):
        cols = [slice(p * D + 128 * j, p * D + 128 * (j + 1)) for p in range(4)]
        tiles = []
        for p in (1, 2, 3):
            v = dot_nn(xin, w_in_ref[:, cols[p]])
            pre[:, cols[p]] = v
            tiles.append(jax.nn.silu(v))
        vt, qt, kt = tiles
        skv[2 * j] = jnp.where(lo, kt, swap(vt)).astype(BF16)
        skv[2 * j + 1] = jnp.where(lo, swap(kt), vt).astype(BF16)
        qt = qt * 0.0625
        sq[2 * j] = pack_rows(qt, 0).astype(BF16)
        sq[2 * j + 1] = pack_rows(qt, 1).astype(BF16)

    negs[:, :D] = neg_ref[...].astype(F32)
    meta_lane = lax.broadcasted_iota(I32, (8, 128), 1)
    meta_row = lax.broadcasted_iota(I32, (8, 128), 0)
    meta = jnp.zeros((8, 128), F32)
    for i in range(8):
        here = meta_lane == b * 8 + i
        meta = meta + jnp.where(
            jnp.logical_and(here, meta_row == 0), nid_ref[i].astype(F32),
            jnp.where(jnp.logical_and(here, meta_row == 1), ncnt_ref[i].astype(F32), 0.0),
        )
    negs[:, D:] = meta

    pl.semaphore_wait(barrier, 1 + (NY - 1) + NY + (NB - 1))

    def kv_copy(d):
        h = yo(d)
        return copy(skv.at[h], kv.at[me], kv_s.at[h], kv_r.at[y], ctx=at(x, h, c))

    def q_copy(d):
        h = yo(d)
        return copy(sq.at[h], rq.at[y], q_s.at[h], q_r.at[y], ctx=at(x, h, c))

    far_first = sorted(range(1, NY), key=lambda d: -min(d, NY - d))
    for d in far_first:
        kv_copy(d).start()
        q_copy(d).start()
    kv[me] = skv[y]
    rq[y] = sq[y]

    def relay(yy):
        r = at(x, yy, c)
        return copy(kv.at[r], kv.at[r], rel_s.at[yy], rel_r.at[yy], ctx=sib)

    def own_relay():
        return copy(skv.at[y], kv.at[me], rel_s.at[y], rel_r.at[y], ctx=sib)

    def forward(yy):
        r = at(0, yy, c)
        return copy(kv.at[r], kv.at[r], xf_s.at[yy], xf_r.at[yy], ctx=at(1, y, c))

    def own_forward():
        return copy(skv.at[y], kv.at[me], xf_s.at[y], xf_r.at[y], ctx=at(1, y, c))

    own_relay().start()

    @pl.when(x == 0)
    def _():
        own_forward().start()

    def neg_copy(d):
        return copy(negs, nega.at[b], neg_s.at[d], neg_r.at[b], batch=bo(d))

    for d in range(1, NB):
        neg_copy(d).start()
    nega[b] = negs[...]

    g_pre = dot_nn(xin, w_in_ref[:, :D])
    pre[:, :D] = g_pre

    near_first = far_first[::-1]
    for d in near_first:
        yy = yo(d)
        copy(skv.at[yy], kv.at[at(x, yy, c)], kv_s.at[yy], kv_r.at[yy], ctx=at(x, yy, c)).wait_recv()
        relay(yy).start()

        @pl.when(x == 0)
        def _():
            forward(yy).start()

    for d in near_first:
        yy = yo(d)
        copy(sq.at[yy], rq.at[yy], q_s.at[yy], q_r.at[yy], ctx=at(x, yy, c)).wait_recv()
    half = low((64, 128))
    for i in range(NY):
        v = rq[i].astype(F32)
        qz[i * 128 : i * 128 + 64] = jnp.where(half, v, 0.0).astype(BF16)
        qz[i * 128 + 64 : i * 128 + 128] = jnp.where(half, swap(v), 0.0).astype(BF16)
    acc[...] = jnp.zeros_like(acc)
    for d in range(NY):
        yy = yo(d)
        r = at(x, yy, 1 - c)
        copy(kv.at[r], kv.at[r], rel_s.at[yy], rel_r.at[yy], ctx=sib).wait_recv()

    def q_rows(k):
        return pl.ds(pl.multiple_of(k * 256, 256), 256)

    def keys_of(t):
        return kv[pl.ds(t * 4, 4)].reshape(512, 128)

    def allowed():
        i = lax.broadcasted_iota(I32, (256, 512), 0)
        j = lax.broadcasted_iota(I32, (256, 512), 1)
        return j <= i + jnp.where(i >= 128, 128, 0) + c * 128

    def fwd(k, t, diagonal):
        tile = keys_of(t)
        h = dot_nt(qz[q_rows(k), :], tile)
        w = h + h * jnp.tanh(h)
        if diagonal:
            w = jnp.where(allowed(), w, 0.0)
        acc[q_rows(k), :] += dot_nn(w.astype(BF16), tile)

    @pl.loop(0, T)
    def _(k):
        fwd(k, x * T + k, True)

        @pl.loop(0, k)
        def _(t):
            fwd(k, x * T + t, False)

    @pl.when(x == 1)
    def _():
        for d in range(NY):
            yy = yo(d)
            r = at(0, yy, c)
            copy(kv.at[r], kv.at[r], xf_s.at[yy], xf_r.at[yy], ctx=at(0, y, c)).wait_recv()
            copy(kv.at[r], kv.at[r], xr_s.at[yy], xr_r.at[yy], ctx=sib).start()
        for d in range(NY):
            yy = yo(d)
            r = at(0, yy, 1 - c)
            copy(kv.at[r], kv.at[r], xr_s.at[yy], xr_r.at[yy], ctx=sib).wait_recv()

        @pl.loop(0, T)
        def _(k):
            @pl.loop(0, T)
            def _(t):
                fwd(k, t, False)

    for i in range(NY):
        top = acc[i * 128 : i * 128 + 64]
        bottom = acc[i * 128 + 64 : i * 128 + 128]
        smix[i] = jnp.where(half, swap(top), bottom).astype(BF16)

    def mix_copy(d):
        yy = yo(d)
        return copy(smix.at[yy], rmix.at[y], mix_s.at[yy], mix_r.at[y], ctx=at(x, yy, c))

    for d in far_first:
        mix_copy(d).start()
    rmix[y] = smix[y]

    for d in range(1, NB):
        bb = bo(d)
        copy(negs, nega.at[bb], neg_s.at[d], neg_r.at[bb], batch=bb).wait_recv()
    NEG = 8 * NB
    neg_f = nega[:, :, :D].reshape(NEG, D)
    neg_b = (neg_f * lax.rsqrt(jnp.sum(neg_f * neg_f, axis=1, keepdims=True) + 1e-06)).astype(BF16)
    metas = nega[0, :, D:]
    for i in range(1, NB):
        metas = metas + nega[i, :, D:]
    ids = metas[0:1, :NEG]
    counts = metas[1:2, :NEG]
    log_share = jnp.log(NEG * counts / jnp.sum(counts, axis=1, keepdims=True))
    pid = jnp.transpose(jnp.broadcast_to(pid_ref[...].astype(F32), (NEG, ROWS)))
    same = pid == ids
    posf = pos_ref[0].astype(F32)
    pos_unit = posf * lax.rsqrt(jnp.sum(posf * posf, axis=1, keepdims=True) + 1e-06)
    gate_u = jax.nn.silu(pre[:, :D]).astype(BF16).astype(F32)

    for d in near_first:
        yy = yo(d)
        copy(smix.at[yy], rmix.at[yy], mix_s.at[yy], mix_r.at[yy], ctx=at(x, yy, c)).wait_recv()
    mixed = jnp.concatenate(
        [unpack_pair(rmix[2 * j].astype(F32), rmix[2 * j + 1].astype(F32)) for j in range(NY // 2)], axis=1
    )
    centred = mixed - jnp.mean(mixed, axis=1, keepdims=True)
    inv_std = lax.rsqrt(jnp.mean(centred * centred, axis=1, keepdims=True) + 1e-05)
    normed = centred * inv_std
    gated = (normed * gate_u).astype(BF16)
    outputs = xin.astype(F32) + dot_nn(gated, w_out_ref[...])
    out_scale = lax.rsqrt(jnp.sum(outputs * outputs, axis=1, keepdims=True) + 1e-06)
    user = outputs * out_scale
    user_b = user.astype(BF16)
    positive = jnp.sum(user * pos_unit, axis=1, keepdims=True) * TEMPER_INV
    logits = dot_nt(user_b, neg_b) * TEMPER_INV - log_share
    terms = jnp.where(same, 0.0, jnp.exp(logits))
    pos_exp = jnp.exp(positive)
    denom = pos_exp + jnp.sum(terms, axis=1, keepdims=True)
    loss = jnp.log(denom) - positive
    d_pos = pos_exp / denom - 1.0
    probs = terms / denom
    probs_b = probs.astype(BF16)
    d_user = (d_pos * TEMPER_INV) * pos_unit + dot_nn(probs_b, neg_b) * TEMPER_INV
    d_out = out_scale * (d_user - user * jnp.sum(user * d_user, axis=1, keepdims=True))
    dout[...] = d_out
    d_gated = dot_nt(d_out.astype(BF16), w_out_ref[...])
    d_normed = d_gated * gate_u
    d_gate = d_gated * normed
    d_mixed = inv_std * (
        d_normed
        - jnp.mean(d_normed, axis=1, keepdims=True)
        - normed * jnp.mean(d_normed * normed, axis=1, keepdims=True)
    )
    for j in range(NY // 2):
        tile = d_mixed[:, 128 * j : 128 * (j + 1)]
        sdm[2 * j] = pack_rows(tile, 0).astype(BF16)
        sdm[2 * j + 1] = pack_rows(tile, 1).astype(BF16)

    def dm_copy(d):
        yy = yo(d)
        return copy(sdm.at[yy], rdm.at[y], dm_s.at[yy], dm_r.at[y], ctx=at(x, yy, c))

    for d in far_first:
        dm_copy(d).start()
    rdm[y] = sdm[y]

    dpre[:, :D] = (d_gate * slope(pre[:, :D])).astype(BF16)
    loss_ref[...] = jnp.transpose(jnp.broadcast_to(loss, (ROWS, 128)))[0:1, :]
    grad = dot_nn(jnp.transpose(probs).astype(BF16), user_b) * TEMPER_INV
    gsend[...] = grad.reshape(NB, 8, D)

    def gb_copy(d):
        bb = bo(d)
        return copy(gsend.at[bb], grecv.at[b], gb_s.at[d], gb_r.at[b], batch=bb)

    for d in range(1, NB):
        gb_copy(d).start()
    grecv[b] = gsend[b]
    dq[...] = jnp.zeros_like(dq)
    dkv[...] = jnp.zeros_like(dkv)

    for d in near_first:
        yy = yo(d)
        copy(sdm.at[yy], rdm.at[yy], dm_s.at[yy], dm_r.at[yy], ctx=at(x, yy, c)).wait_recv()
    for i in range(NY):
        v = rdm[i].astype(F32)
        up = jnp.concatenate([jnp.where(half, 0.0, swap(v)), jnp.where(half, 0.0, v)], axis=0)
        dmz[i * 128 : i * 128 + 128] = up.astype(BF16)
        both = up + qz[i * 128 : i * 128 + 128].astype(F32)
        qdt[i // 2, :, 128 * (i % 2) : 128 * (i % 2) + 128] = jnp.transpose(both).astype(BF16)

    def bwd(k, t, diagonal):
        tile = keys_of(t)
        h = dot_nt(qz[q_rows(k), :], tile)
        dw = dot_nt(dmz[q_rows(k), :], tile)
        th = jnp.tanh(h)
        u = 1.0 + th
        w = h * u
        ds = dw * (u + w * (1.0 - th))
        if diagonal:
            ok = allowed()
            w = jnp.where(ok, w, 0.0)
            ds = jnp.where(ok, ds, 0.0)
        w = w.astype(BF16)
        ds = ds.astype(BF16)
        dq[q_rows(k), :] += dot_nn(ds, tile)
        dk = dot_nn(qdt[k, :64, :], ds)
        dv = dot_nn(qdt[k, 64:, :], w)
        for j in range(4):
            dkv[t * 4 + j, :64, :] += dk[:, 128 * j : 128 * (j + 1)]
            dkv[t * 4 + j, 64:, :] += dv[:, 128 * j : 128 * (j + 1)]

    def sib_own(yy):
        return copy(dkv.at[at(x, yy, 1 - c)], sibo.at[yy], so_s.at[yy], so_r.at[yy], ctx=sib)

    def sib_cross(yy):
        return copy(dkv.at[at(0, yy, 1 - c)], sibx.at[yy], sx_s.at[yy], sx_r.at[yy], ctx=sib)

    def cross(yy):
        return copy(sx.at[yy], rx.at[yy], xx_s.at[yy], xx_r.at[yy], ctx=at(1 - x, y, c))

    @pl.when(x == 1)
    def _():
        @pl.loop(0, T)
        def _(t):
            @pl.loop(0, T)
            def _(k):
                bwd(k, t, False)

        for i in range(NY):
            sib_cross(i).start()
        for i in range(NY):
            sib_cross(i).wait_recv()
            sx[i] = (dkv[at(0, i, c)] + sibx[i]).astype(BF16)
            cross(i).start()

    @pl.loop(0, T)
    def _(t):
        bwd(t, x * T + t, True)

        @pl.loop(t + 1, T)
        def _(k):
            bwd(k, x * T + t, False)

    for i in range(NY):
        sib_own(i).start()

    for i in range(NY):
        top = dq[i * 128 : i * 128 + 64] * 0.0625
        bottom = dq[i * 128 + 64 : i * 128 + 128] * 0.0625
        sretq[i] = jnp.where(half, top, swap(bottom)).astype(BF16)

    def retq_copy(d):
        yy = yo(d)
        return copy(sretq.at[yy], rretq.at[y], retq_s.at[yy], retq_r.at[y], ctx=at(x, yy, c))

    for d in far_first:
        retq_copy(d).start()
    rretq[y] = sretq[y]

    for d in range(1, NB):
        bb = bo(d)
        copy(gsend.at[bb], grecv.at[bb], gb_s.at[d], gb_r.at[bb], batch=bb).wait_recv()
    g1[...] = jnp.sum(grecv[...], axis=0)

    def g1_copy():
        return copy(g1, g2, g1_s.at[0], g1_r.at[0], ctx=sib)

    g1_copy().start()

    def ret_copy(d):
        yy = yo(d)
        return copy(sret.at[yy], rret.at[y], ret_s.at[yy], ret_r.at[y], ctx=at(x, yy, c))

    for d in far_first + [0]:
        yy = yo(d)
        sib_own(yy).wait_recv()
        total = dkv[at(x, yy, c)] + sibo[yy]

        @pl.when(x == 0)
        def _():
            copy(sx.at[yy], rx.at[yy], xx_s.at[yy], xx_r.at[yy], ctx=at(1, y, c)).wait_recv()
            sret[yy] = jnp.transpose(total + rx[yy].astype(F32)).astype(BF16)

        @pl.when(x == 1)
        def _():
            sret[yy] = jnp.transpose(total).astype(BF16)

        if d:
            ret_copy(d).start()
    rret[y] = sret[y]

    g1_copy().wait_recv()
    H = D // 2
    gsum = g1[...] + g2[...]
    g3[...] = jnp.where(c == 0, gsum[:, :H], gsum[:, H:])

    def gc_copy(d, xx):
        yy = yo(d)
        return copy(g3, g4.at[x * NY + y], gc_s.at[xx * NY + d], gc_r.at[x * NY + y], ctx=at(jnp.where(xx == 0, x, 1 - x), yy, c))

    peers = [(d, 0) for d in range(1, NY)] + [(d, 1) for d in range(NY)]
    for d, xx in peers:
        gc_copy(d, xx).start()
    g4[x * NY + y] = g3[...]

    for d in near_first:
        yy = yo(d)
        copy(sretq.at[yy], rretq.at[yy], retq_s.at[yy], retq_r.at[yy], ctx=at(x, yy, c)).wait_recv()
    for j in range(NY // 2):
        cols = slice(2 * D + 128 * j, 2 * D + 128 * (j + 1))
        d_q = unpack_pair(rretq[2 * j].astype(F32), rretq[2 * j + 1].astype(F32))
        dpre[:, cols] = (d_q * slope(pre[:, cols])).astype(BF16)

    for d, xx in peers:
        s = jnp.where(xx == 0, x, 1 - x) * NY + yo(d)
        copy(g3, g4.at[s], gc_s.at[xx * NY + d], gc_r.at[s], ctx=sib).wait_recv()
    gfin[c] = jnp.sum(g4[...], axis=0)

    def g4_copy():
        return copy(gfin.at[c], gfin.at[c], g4_s.at[0], g4_r.at[0], ctx=sib)

    g4_copy().start()

    for d in near_first:
        yy = yo(d)
        copy(sret.at[yy], rret.at[yy], ret_s.at[yy], ret_r.at[yy], ctx=at(x, yy, c)).wait_recv()
    for j in range(NY // 2):
        even, odd = rret[2 * j].astype(F32), rret[2 * j + 1].astype(F32)
        cols = slice(3 * D + 128 * j, 3 * D + 128 * (j + 1))
        dpre[:, cols] = (jnp.where(lo, even, swap(odd)) * slope(pre[:, cols])).astype(BF16)
        cols = slice(D + 128 * j, D + 128 * (j + 1))
        dpre[:, cols] = (jnp.where(lo, swap(even), odd) * slope(pre[:, cols])).astype(BF16)
    dseq_ref[0] = (dout[...] + dot_nt(dpre[...], w_in_ref[...])).astype(BF16)

    copy(gfin.at[1 - c], gfin.at[1 - c], g4_s.at[0], g4_r.at[0], ctx=sib).wait_recv()
    d_total = jnp.concatenate([gfin[0], gfin[1]], axis=1)
    nf = neg_ref[...].astype(F32)
    scale = lax.rsqrt(jnp.sum(nf * nf, axis=1, keepdims=True) + 1e-06)
    unit = nf * scale
    dneg_ref[...] = scale * (d_total - unit * jnp.sum(unit * d_total, axis=1, keepdims=True))

    for d in range(1, NY):
        kv_copy(d).wait_send()
        q_copy(d).wait_send()
        mix_copy(d).wait_send()
        dm_copy(d).wait_send()
        retq_copy(d).wait_send()
        ret_copy(d).wait_send()
    for i in range(NY):
        relay(i).wait_send()
        sib_own(i).wait_send()
    for d in range(1, NB):
        neg_copy(d).wait_send()
        gb_copy(d).wait_send()
    for d, xx in peers:
        gc_copy(d, xx).wait_send()
    g1_copy().wait_send()
    g4_copy().wait_send()

    @pl.when(x == 0)
    def _():
        for i in range(NY):
            forward(i).wait_send()

    @pl.when(x == 1)
    def _():
        for i in range(NY):
            r = at(0, i, c)
            copy(kv.at[r], kv.at[r], xr_s.at[i], xr_r.at[i], ctx=sib).wait_send()
            sib_cross(i).wait_send()
            cross(i).wait_send()


def solution(mesh):
    NY = mesh.shape["ctx"] // 4
    NB = mesh.shape["batch"]
    D = HEAD * NY
    V, S = pltpu.VMEM, pltpu.SemaphoreType.DMA

    def body(*refs):
        kernel(NY, NB, *refs)

    def shards(seq_in, w_in, w_out, pos_emb, pos_ids, neg_emb, neg_ids, neg_counts):
        vm = pl.BlockSpec(memory_space=pltpu.VMEM)
        sm = pl.BlockSpec(memory_space=pltpu.SMEM)
        return pl.pallas_call(
            body,
            out_shape=(
                jax.ShapeDtypeStruct((1, ROWS), F32),
                jax.ShapeDtypeStruct((1, ROWS, D), BF16),
                jax.ShapeDtypeStruct((8, D), F32),
            ),
            in_specs=[vm] * 6 + [sm] * 2,
            out_specs=(vm, vm, vm),
            scratch_shapes=[
                V((ROWS, 4 * D), F32),
                V((NY, 128, 128), BF16),
                V((NY, 64, 128), BF16),
                V((4 * NY, 128, 128), BF16),
                V((NY, 64, 128), BF16),
                V((NY * 128, 128), BF16),
                V((NY * 128, 128), F32),
                V((NY, 64, 128), BF16),
                V((NY, 64, 128), BF16),
                V((NY, 64, 128), BF16),
                V((NY, 64, 128), BF16),
                V((NY * 128, 128), BF16),
                V((NY // 2, 128, 256), BF16),
                V((NY * 128, 128), F32),
                V((4 * NY, 128, 128), F32),
                V((NY, 128, 128), F32),
                V((NY, 128, 128), F32),
                V((NY, 128, 128), BF16),
                V((NY, 128, 128), BF16),
                V((NY, 128, 128), BF16),
                V((NY, 128, 128), BF16),
                V((NY, 64, 128), BF16),
                V((NY, 64, 128), BF16),
                V((ROWS, D), F32),
                V((ROWS, 4 * D), BF16),
                V((8, D + 128), F32),
                V((NB, 8, D + 128), F32),
                V((NB, 8, D), F32),
                V((NB, 8, D), F32),
                V((8, D), F32),
                V((8, D), F32),
                V((8, D // 2), F32),
                V((2 * NY, 8, D // 2), F32),
                V((2, 8, D // 2), F32),
            ]
            + [S((NY,))] * 24
            + [S((NB,))] * 4
            + [S((1,))] * 2
            + [S((2 * NY,))] * 2
            + [S((1,))] * 2,
            compiler_params=pltpu.CompilerParams(
                collective_id=0, has_side_effects=True, vmem_limit_bytes=48 << 20
            ),
        )(seq_in, w_in, w_out, pos_emb, pos_ids, neg_emb, neg_ids, neg_counts)

    in_specs = (
        P("batch", "ctx", None), P(), P(), P("batch", "ctx", None), P("batch", "ctx"),
        P("batch", None), P("batch"), P("batch"),
    )
    out_specs = (P("batch", "ctx"), P("batch", "ctx", None), P("batch", None))
    return jax.shard_map(shards, mesh=mesh, in_specs=in_specs, out_specs=out_specs, check_vma=False)
```

time: 610 us -> 96.4 us (0.16)
  waiting for transfers between devices: 194 us -> 0 us
  blocking collectives: 171 us -> 0 us
  matrix products: 158 us -> 0 us
  Pallas kernels: 0 us -> 86.6 us
  local copies, waits for them, and re-layouts: 52.5 us -> 8.87 us
  other arithmetic: 15.9 us -> 0 us
  between operations: 14.8 us -> 0.66 us
    all_gather x4 -> x0, waiting for transfers between devices: 193 us -> none  [the longest x1 86.6 us: shards(): lax.all_gather(key_rows, 'ctx', axis=0, tiled=True)]
    dot_general x55 -> x0, matrix products: 158 us -> none  [the longest x8 29.6 us: inner_step(): jnp.einsum('hij,ihe->jhe', d_scores, query_blk, preferred_element_type=jn...]
    psum x1 -> x0, blocking collectives: 125 us -> none  [shards(): d_total = lax.psum(owned, 'ctx')]
    pallas_call x0 -> x1, Pallas kernels: none -> 86.6 us  [shards(): pl.pallas_call(body, out_shape=(jax.ShapeDtypeStruct((1, ROWS), F32), jax...]
    all_gather x1 -> x0, blocking collectives: 26.8 us -> none  [shards(): lax.all_gather(neg_unit.astype(jnp.bfloat16), 'batch', axis=0, tiled=True)]
    dynamic_slice x24 -> x0, local copies, waits for them, and re-layouts: 19.9 us -> none  [the longest x16 11.8 us: inner_step(): lax.dynamic_slice_in_dim(grads_piece, first, inner, 0)]
    unnamed x1 -> x0, blocking collectives: 19.5 us -> none
    all_gather x2 -> x0, local copies, waits for them, and re-layouts: 12.8 us -> none  [the longest x1 6.39 us: shards(): lax.all_gather(key_rows, 'ctx', axis=0, tiled=True)]
  transfers between devices with their start and end apart: 5 -> 0, of which waited for: 3 -> 0; matrix products, arithmetic and copies ran while one was open for 12% -> 0% of each run, Pallas kernels for 0% -> 0%
where the time goes in v1:
time: 96.4 us; the launch traced here: 96.1 us
  Pallas kernels  86.6 us (90%)
  local copies, waits for them, and re-layouts  8.87 us (9%)
    pallas_call x1, Pallas kernels, shards(): pl.pallas_call(body, out_shape=(jax.ShapeDtypeStruct((1, ROWS), F32), jax...  86.6 us
    unnamed x19, local copies, waits for them, and re-layouts  8.87 us

profile of v1, /device:TPU:1, one launch (start us, length us, event | category | flops | bytes accessed | tf_op | source)
XLA Modules:
  0.0 96.1 jit_solution(4266993151540592870)
XLA Ops:
  0.6 0.0 copy-start
  0.6 1.6 %copy-done = bf16[512,2048]{1,0:T(8,128)(2,1)S(1)} copy-done((bf16[512,2048]{1,0:T(8,128)(2,1)S(1)}, bf16[512,2048]{1,0:T(8,128)(2,1)}, u32[]{:S(2)}) %copy-start) | copy-done | bytes 2097176
  2.2 0.0 copy-start.1
  2.2 1.0 %copy-done.1 = bf16[512,512]{1,0:T(8,128)(2,1)S(1)} copy-done((bf16[512,512]{1,0:T(8,128)(2,1)S(1)}, bf16[512,512]{1,0:T(8,128)(2,1)}, u32[]{:S(2)}) %copy-start.1) | copy-done | bytes 524312
  3.3 0.0 copy-start.2
  3.3 0.9 copy-done.2
  4.2 0.0 copy-start.3
  4.2 0.9 copy-done.3
  5.1 0.0 copy-start.4
  5.1 0.7 copy-done.4
  5.8 0.0 copy-start.5
  5.8 0.7 copy-done.5
  6.4 0.0 copy-start.6
  6.4 0.7 copy-done.6
  7.1 0.0 copy-start.7
  7.1 0.7 copy-done.7
  7.7 86.6 %shard_map.103 = (f32[1,128]{1,0:T(1,128)S(1)}, bf16[1,128,512]{2,1,0:T(8,128)(2,1)S(1)}, f32[8,512]{1,0:T(8,128)S(1)}) custom-call(bf16[1,128,512]{2,1,0:T(8,128)(2,1)S(1)} %copy-done.2, bf16[512,2048]{1,0:T(8,128)(2,1)S(1)} %copy-done, bf16[512,512]{1,0:T(8,128)(2,1)S(1)} %copy-done.1, bf16[1,128,512]{2,1,0:T(8,128)(2,1)S(1)} %copy-done.3, ...), custom_call_target="tpu_custom_call" | custom-call | tf_op jit(solution)/shard_map/pallas_call | solution.py:536
  94.3 0.5 copy.14
  94.8 0.7 copy.15
  95.5 0.6 copy.16
Async XLA Ops:
  0.6 1.6 %copy-start = (bf16[512,2048]{1,0:T(8,128)(2,1)S(1)}, bf16[512,2048]{1,0:T(8,128)(2,1)}, u32[]{:S(2)}) copy-start(bf16[512,2048]{1,0:T(8,128)(2,1)} %refs_1_.1) | copy-start | bytes 6291460
  2.2 1.0 %copy-start.1 = (bf16[512,512]{1,0:T(8,128)(2,1)S(1)}, bf16[512,512]{1,0:T(8,128)(2,1)}, u32[]{:S(2)}) copy-start(bf16[512,512]{1,0:T(8,128)(2,1)} %refs_2_.1) | copy-start | bytes 1572868
  3.3 0.9 copy-start.2
  4.2 0.9 copy-start.3
  5.1 0.7 copy-start.4
  5.8 0.7 copy-start.5
  6.4 0.7 copy-start.6
  7.1 0.7 copy-start.7

commit v2 on v1

--- a/solution.py
+++ b/solution.py
@@ -48,8 +48,9 @@
 
 def kernel(
     NY, NB,
-    seq_ref, w_in_ref, w_out_ref, pos_ref, pid_ref, neg_ref, nid_ref, ncnt_ref,
+    seq_hbm, w_in_hbm, w_out_hbm, pos_hbm, pid_hbm, neg_hbm, nid_hbm, ncnt_hbm,
     loss_ref, dseq_ref, dneg_ref,
+    seq_ref, w_in_ref, w_out_ref, pos_ref, pid_ref, neg_ref, nid_ref, ncnt_ref, in_s,
     pre, skv, sq, kv, rq, qz, acc, smix, rmix, sdm, rdm, dmz, qdt, dq, dkv,
     sibo, sibx, sx, rx, sret, rret, sretq, rretq, dout, dpre, negs, nega, gsend, grecv, g1, g2, g3, g4, gfin,
     kv_s, kv_r, q_s, q_r, rel_s, rel_r, xf_s, xf_r, xr_s, xr_r, mix_s, mix_r, dm_s, dm_r,
@@ -83,12 +84,33 @@
             src_ref=src, dst_ref=dst, send_sem=ss, recv_sem=rs, device_id=where, device_id_type=MESH
         )
 
+
+    loads = [
+        pltpu.make_async_copy(src, dst, in_s.at[i])
+        for i, (src, dst) in enumerate(
+            [
+                (seq_hbm, seq_ref),
+                (w_in_hbm.at[:, D:], w_in_ref.at[:, D:]),
+                (w_in_hbm.at[:, :D], w_in_ref.at[:, :D]),
+                (neg_hbm, neg_ref),
+                (nid_hbm, nid_ref),
+                (ncnt_hbm, ncnt_ref),
+                (pos_hbm, pos_ref),
+                (pid_hbm, pid_ref),
+                (w_out_hbm, w_out_ref),
+            ]
+        )
+    ]
+    for load in loads:
+        load.start()
     barrier = pltpu.get_barrier_semaphore()
     for p in [sib] + others + across:
         pl.semaphore_signal(barrier, inc=1, device_id={"ctx": p}, device_id_type=MESH)
     for d in range(1, NB):
         pl.semaphore_signal(barrier, inc=1, device_id={"batch": bo(d)}, device_id_type=MESH)
 
+    loads[0].wait()
+    loads[1].wait()
     xin = seq_ref[0]
     lane = lax.broadcasted_iota(I32, (ROWS, 128), 1)
     lo = lane < HEAD
@@ -107,6 +129,8 @@
         sq[2 * j] = pack_rows(qt, 0).astype(BF16)
         sq[2 * j + 1] = pack_rows(qt, 1).astype(BF16)
 
+    for load in loads[2:]:
+        load.wait()
     negs[:, :D] = neg_ref[...].astype(F32)
     meta_lane = lax.broadcasted_iota(I32, (8, 128), 1)
     meta_row = lax.broadcasted_iota(I32, (8, 128), 0)
@@ -184,14 +208,10 @@
         v = rq[i].astype(F32)
         qz[i * 128 : i * 128 + 64] = jnp.where(half, v, 0.0).astype(BF16)
         qz[i * 128 + 64 : i * 128 + 128] = jnp.where(half, swap(v), 0.0).astype(BF16)
-    acc[...] = jnp.zeros_like(acc)
     for d in range(NY):
         yy = yo(d)
         r = at(x, yy, 1 - c)
         copy(kv.at[r], kv.at[r], rel_s.at[yy], rel_r.at[yy], ctx=sib).wait_recv()
-
-    def q_rows(k):
-        return pl.ds(pl.multiple_of(k * 256, 256), 256)
 
     def keys_of(t):
         return kv[pl.ds(t * 4, 4)].reshape(512, 128)
@@ -201,52 +221,71 @@
         j = lax.broadcasted_iota(I32, (256, 512), 1)
         return j <= i + jnp.where(i >= 128, 128, 0) + c * 128
 
-    def fwd(k, t, diagonal):
-        tile = keys_of(t)
-        h = dot_nt(qz[q_rows(k), :], tile)
+    def weighted(q, tile, diagonal):
+        h = dot_nt(q, tile)
         w = h + h * jnp.tanh(h)
         if diagonal:
-            w = jnp.where(allowed(), w, 0.0)
-        acc[q_rows(k), :] += dot_nn(w.astype(BF16), tile)
-
-    @pl.loop(0, T)
-    def _(k):
-        fwd(k, x * T + k, True)
-
-        @pl.loop(0, k)
-        def _(t):
-            fwd(k, x * T + t, False)
+            last = jnp.where(allowed(), w[:, -512:], 0.0)
+            w = last if w.shape[1] == 512 else jnp.concatenate([w[:, :-512], last], axis=1)
+        return dot_nn(w.astype(BF16), tile)
+
+    def mix_copy(i):
+        return copy(smix.at[i], rmix.at[y], mix_s.at[i], mix_r.at[y], ctx=at(x, i, c))
+
+    def send_mixed(k, rows):
+        for e in range(2):
+            i = 2 * k + e
+            top, bottom = rows[e * 128 : e * 128 + 64], rows[e * 128 + 64 : e * 128 + 128]
+            smix[i] = jnp.where(half, swap(top), bottom).astype(BF16)
+
+            @pl.when(y == i)
+            def _():
+                rmix[y] = smix[i]
+
+            @pl.when(y != i)
+            def _():
+                mix_copy(i).start()
+
+    def cross_in(yy):
+        r = at(0, yy, c)
+        return copy(kv.at[r], kv.at[r], xf_s.at[yy], xf_r.at[yy], ctx=at(1 - x, y, c))
+
+    def cross_relay(yy, cc):
+        r = at(0, yy, cc)
+        return copy(kv.at[r], kv.at[r], xr_s.at[yy], xr_r.at[yy], ctx=sib)
+
+    def take_cross(ds):
+        @pl.when(x == 1)
+        def _():
+            for d in ds:
+                cross_in(yo(d)).wait_recv()
+                cross_relay(yo(d), c).start()
+
+    order = [0] + near_first
+    take_cross(order[: NY // 2])
+    for k in range(T):
+        if k == T - 1:
+            take_cross(order[NY // 2 :])
+        tile = kv[pl.ds(x * 2 * NY, 4 * (k + 1))].reshape(512 * (k + 1), 128)
+        rows = weighted(qz[256 * k : 256 * (k + 1)], tile, True)
+
+        @pl.when(x == 0)
+        def _():
+            send_mixed(k, rows)
+
+        @pl.when(x == 1)
+        def _():
+            acc[256 * k : 256 * (k + 1)] = rows
+
 
     @pl.when(x == 1)
     def _():
-        for d in range(NY):
-            yy = yo(d)
-            r = at(0, yy, c)
-            copy(kv.at[r], kv.at[r], xf_s.at[yy], xf_r.at[yy], ctx=at(0, y, c)).wait_recv()
-            copy(kv.at[r], kv.at[r], xr_s.at[yy], xr_r.at[yy], ctx=sib).start()
-        for d in range(NY):
-            yy = yo(d)
-            r = at(0, yy, 1 - c)
-            copy(kv.at[r], kv.at[r], xr_s.at[yy], xr_r.at[yy], ctx=sib).wait_recv()
-
-        @pl.loop(0, T)
-        def _(k):
-            @pl.loop(0, T)
-            def _(t):
-                fwd(k, t, False)
-
-    for i in range(NY):
-        top = acc[i * 128 : i * 128 + 64]
-        bottom = acc[i * 128 + 64 : i * 128 + 128]
-        smix[i] = jnp.where(half, swap(top), bottom).astype(BF16)
-
-    def mix_copy(d):
-        yy = yo(d)
-        return copy(smix.at[yy], rmix.at[y], mix_s.at[yy], mix_r.at[y], ctx=at(x, yy, c))
-
-    for d in far_first:
-        mix_copy(d).start()
-    rmix[y] = smix[y]
+        for d in order:
+            cross_relay(yo(d), 1 - c).wait_recv()
+        tile = kv[: 2 * NY].reshape(512 * T, 128)
+        for k in range(T):
+            rows = slice(256 * k, 256 * (k + 1))
+            send_mixed(k, acc[rows] + weighted(qz[rows], tile, False))
 
     for d in range(1, NB):
         bb = bo(d)
@@ -291,7 +330,6 @@
     probs_b = probs.astype(BF16)
     d_user = (d_pos * TEMPER_INV) * pos_unit + dot_nn(probs_b, neg_b) * TEMPER_INV
     d_out = out_scale * (d_user - user * jnp.sum(user * d_user, axis=1, keepdims=True))
-    dout[...] = d_out
     d_gated = dot_nt(d_out.astype(BF16), w_out_ref[...])
     d_normed = d_gated * gate_u
     d_gate = d_gated * normed
@@ -313,7 +351,8 @@
         dm_copy(d).start()
     rdm[y] = sdm[y]
 
-    dpre[:, :D] = (d_gate * slope(pre[:, :D])).astype(BF16)
+    d_pre = (d_gate * slope(pre[:, :D])).astype(BF16)
+    dout[...] = d_out + dot_nt(d_pre, w_in_ref[:, :D])
     loss_ref[...] = jnp.transpose(jnp.broadcast_to(loss, (ROWS, 128)))[0:1, :]
     grad = dot_nn(jnp.transpose(probs).astype(BF16), user_b) * TEMPER_INV
     gsend[...] = grad.reshape(NB, 8, D)
@@ -326,7 +365,6 @@
         gb_copy(d).start()
     grecv[b] = gsend[b]
     dq[...] = jnp.zeros_like(dq)
-    dkv[...] = jnp.zeros_like(dkv)
 
     for d in near_first:
         yy = yo(d)
@@ -336,28 +374,70 @@
         up = jnp.concatenate([jnp.where(half, 0.0, swap(v)), jnp.where(half, 0.0, v)], axis=0)
         dmz[i * 128 : i * 128 + 128] = up.astype(BF16)
         both = up + qz[i * 128 : i * 128 + 128].astype(F32)
-        qdt[i // 2, :, 128 * (i % 2) : 128 * (i % 2) + 128] = jnp.transpose(both).astype(BF16)
-
-    def bwd(k, t, diagonal):
+        qdt[:, i * 128 : i * 128 + 128] = jnp.transpose(both).astype(BF16)
+
+    def g1_copy():
+        return copy(g1, g2, g1_s.at[0], g1_r.at[0], ctx=sib)
+
+    def gc_copy(d, xx):
+        there = x if xx == 0 else 1 - x
+        return copy(
+            g3, g4.at[x * NY + y], gc_s.at[xx * NY + d], gc_r.at[x * NY + y], ctx=at(there, yo(d), c)
+        )
+
+    def g4_copy():
+        return copy(gfin.at[c], gfin.at[c], g4_s.at[0], g4_r.at[0], ctx=sib)
+
+    peers = [(d, 0) for d in range(1, NY)] + [(d, 1) for d in range(NY)]
+    H = D // 2
+
+    def g_histories():
+        for d in range(1, NB):
+            bb = bo(d)
+            copy(gsend.at[bb], grecv.at[bb], gb_s.at[d], gb_r.at[bb], batch=bb).wait_recv()
+        g1[...] = jnp.sum(grecv[...], axis=0)
+        g1_copy().start()
+
+    def g_pair():
+        g1_copy().wait_recv()
+        gsum = g1[...] + g2[...]
+        g3[...] = jnp.where(c == 0, gsum[:, :H], gsum[:, H:])
+        for d, xx in peers:
+            gc_copy(d, xx).start()
+        g4[x * NY + y] = g3[...]
+
+    def g_chips():
+        for d, xx in peers:
+            s = (x if xx == 0 else 1 - x) * NY + yo(d)
+            copy(g3, g4.at[s], gc_s.at[xx * NY + d], gc_r.at[s], ctx=sib).wait_recv()
+        gfin[c] = jnp.sum(g4[...], axis=0)
+        g4_copy().start()
+
+    def bwd(k0, t, diagonal):
+        rows = slice(256 * k0, 256 * T)
         tile = keys_of(t)
-        h = dot_nt(qz[q_rows(k), :], tile)
-        dw = dot_nt(dmz[q_rows(k), :], tile)
+        h = dot_nt(qz[rows], tile)
+        dw = dot_nt(dmz[rows], tile)
         th = jnp.tanh(h)
         u = 1.0 + th
         w = h * u
         ds = dw * (u + w * (1.0 - th))
         if diagonal:
             ok = allowed()
-            w = jnp.where(ok, w, 0.0)
-            ds = jnp.where(ok, ds, 0.0)
+
+            def masked(v):
+                first = jnp.where(ok, v[:256], 0.0)
+                return first if v.shape[0] == 256 else jnp.concatenate([first, v[256:]], axis=0)
+
+            w, ds = masked(w), masked(ds)
         w = w.astype(BF16)
         ds = ds.astype(BF16)
-        dq[q_rows(k), :] += dot_nn(ds, tile)
-        dk = dot_nn(qdt[k, :64, :], ds)
-        dv = dot_nn(qdt[k, 64:, :], w)
+        dq[rows] += dot_nn(ds, tile)
+        dk = dot_nn(qdt[:64, rows], ds)
+        dv = dot_nn(qdt[64:, rows], w)
         for j in range(4):
-            dkv[t * 4 + j, :64, :] += dk[:, 128 * j : 128 * (j + 1)]
-            dkv[t * 4 + j, 64:, :] += dv[:, 128 * j : 128 * (j + 1)]
+            dkv[t * 4 + j, :64, :] = dk[:, 128 * j : 128 * (j + 1)]
+            dkv[t * 4 + j, 64:, :] = dv[:, 128 * j : 128 * (j + 1)]
 
     def sib_own(yy):
         return copy(dkv.at[at(x, yy, 1 - c)], sibo.at[yy], so_s.at[yy], so_r.at[yy], ctx=sib)
@@ -367,91 +447,97 @@
 
     def cross(yy):
         return copy(sx.at[yy], rx.at[yy], xx_s.at[yy], xx_r.at[yy], ctx=at(1 - x, y, c))
+
+    def cross_sums(t):
+        for e in range(2):
+            i = 2 * t + e
+            sib_cross(i).wait_recv()
+            sx[i] = (dkv[at(0, i, c)] + sibx[i]).astype(BF16)
+            cross(i).start()
+
+    def retq_copy(i):
+        return copy(sretq.at[i], rretq.at[y], retq_s.at[i], retq_r.at[y], ctx=at(x, i, c))
+
+    def ret_copy(i):
+        return copy(sret.at[i], rret.at[y], ret_s.at[i], ret_r.at[y], ctx=at(x, i, c))
+
+    def send_dq(k):
+        for i in (2 * k, 2 * k + 1):
+            top = dq[i * 128 : i * 128 + 64] * 0.0625
+            bottom = dq[i * 128 + 64 : i * 128 + 128] * 0.0625
+            sretq[i] = jnp.where(half, top, swap(bottom)).astype(BF16)
+
+            @pl.when(y == i)
+            def _():
+                rretq[y] = sretq[i]
+
+            @pl.when(y != i)
+            def _():
+                retq_copy(i).start()
+
+    def send_dkv(t, crossed):
+        for i in (2 * t, 2 * t + 1):
+            sib_own(i).wait_recv()
+            total = dkv[at(x, i, c)] + sibo[i]
+            if crossed:
+                cross(i).wait_recv()
+                total = total + rx[i].astype(F32)
+            sret[i] = jnp.transpose(total).astype(BF16)
+
+            @pl.when(y == i)
+            def _():
+                rret[y] = sret[i]
+
+            @pl.when(y != i)
+            def _():
+                ret_copy(i).start()
+
 
     @pl.when(x == 1)
     def _():
         @pl.loop(0, T)
         def _(t):
-            @pl.loop(0, T)
-            def _(k):
-                bwd(k, t, False)
-
-        for i in range(NY):
-            sib_cross(i).start()
-        for i in range(NY):
-            sib_cross(i).wait_recv()
-            sx[i] = (dkv[at(0, i, c)] + sibx[i]).astype(BF16)
-            cross(i).start()
-
-    @pl.loop(0, T)
-    def _(t):
+            bwd(0, t, False)
+            for e in range(2):
+                sib_cross(2 * t + e).start()
+
+            @pl.when(t > 0)
+            def _():
+                cross_sums(t - 1)
+
+    steps = [T - 1] + list(range(T - 1))
+    for n, t in enumerate(steps):
         bwd(t, x * T + t, True)
-
-        @pl.loop(t + 1, T)
-        def _(k):
-            bwd(k, x * T + t, False)
-
-    for i in range(NY):
-        sib_own(i).start()
-
-    for i in range(NY):
-        top = dq[i * 128 : i * 128 + 64] * 0.0625
-        bottom = dq[i * 128 + 64 : i * 128 + 128] * 0.0625
-        sretq[i] = jnp.where(half, top, swap(bottom)).astype(BF16)
-
-    def retq_copy(d):
-        yy = yo(d)
-        return copy(sretq.at[yy], rretq.at[y], retq_s.at[yy], retq_r.at[y], ctx=at(x, yy, c))
-
-    for d in far_first:
-        retq_copy(d).start()
-    rretq[y] = sretq[y]
-
-    for d in range(1, NB):
-        bb = bo(d)
-        copy(gsend.at[bb], grecv.at[bb], gb_s.at[d], gb_r.at[bb], batch=bb).wait_recv()
-    g1[...] = jnp.sum(grecv[...], axis=0)
-
-    def g1_copy():
-        return copy(g1, g2, g1_s.at[0], g1_r.at[0], ctx=sib)
-
-    g1_copy().start()
-
-    def ret_copy(d):
-        yy = yo(d)
-        return copy(sret.at[yy], rret.at[y], ret_s.at[yy], ret_r.at[y], ctx=at(x, yy, c))
-
-    for d in far_first + [0]:
-        yy = yo(d)
-        sib_own(yy).wait_recv()
-        total = dkv[at(x, yy, c)] + sibo[yy]
-
-        @pl.when(x == 0)
-        def _():
-            copy(sx.at[yy], rx.at[yy], xx_s.at[yy], xx_r.at[yy], ctx=at(1, y, c)).wait_recv()
-            sret[yy] = jnp.transpose(total + rx[yy].astype(F32)).astype(BF16)
-
-        @pl.when(x == 1)
-        def _():
-            sret[yy] = jnp.transpose(total).astype(BF16)
-
-        if d:
-            ret_copy(d).start()
-    rret[y] = sret[y]
-
-    g1_copy().wait_recv()
-    H = D // 2
-    gsum = g1[...] + g2[...]
-    g3[...] = jnp.where(c == 0, gsum[:, :H], gsum[:, H:])
-
-    def gc_copy(d, xx):
-        yy = yo(d)
-        return copy(g3, g4.at[x * NY + y], gc_s.at[xx * NY + d], gc_r.at[x * NY + y], ctx=at(jnp.where(xx == 0, x, 1 - x), yy, c))
-
-    peers = [(d, 0) for d in range(1, NY)] + [(d, 1) for d in range(NY)]
-    for d, xx in peers:
-        gc_copy(d, xx).start()
-    g4[x * NY + y] = g3[...]
+        for i in (2 * t, 2 * t + 1):
+            sib_own(i).start()
+        if n == 0:
+
+            @pl.when(x == 1)
+            def _():
+                cross_sums(T - 1)
+
+            g_histories()
+        else:
+            send_dq(t)
+
+            @pl.when(x == 1)
+            def _():
+                send_dkv(steps[n - 1], False)
+        if n == 1 or T == 1:
+            g_pair()
+    send_dq(T - 1)
+
+
+    @pl.when(x == 1)
+    def _():
+        send_dkv(steps[-1], False)
+
+    @pl.when(x == 0)
+    def _():
+        for t in range(T):
+            send_dkv(t, True)
+
+    g_chips()
 
     for d in near_first:
         yy = yo(d)
@@ -460,16 +546,14 @@
         cols = slice(2 * D + 128 * j, 2 * D + 128 * (j + 1))
         d_q = unpack_pair(rretq[2 * j].astype(F32), rretq[2 * j + 1].astype(F32))
         dpre[:, cols] = (d_q * slope(pre[:, cols])).astype(BF16)
-
-    for d, xx in peers:
-        s = jnp.where(xx == 0, x, 1 - x) * NY + yo(d)
-        copy(g3, g4.at[s], gc_s.at[xx * NY + d], gc_r.at[s], ctx=sib).wait_recv()
-    gfin[c] = jnp.sum(g4[...], axis=0)
-
-    def g4_copy():
-        return copy(gfin.at[c], gfin.at[c], g4_s.at[0], g4_r.at[0], ctx=sib)
-
-    g4_copy().start()
+    dout[...] += dot_nt(dpre[:, 2 * D : 3 * D], w_in_ref[:, 2 * D : 3 * D])
+
+    copy(gfin.at[1 - c], gfin.at[1 - c], g4_s.at[0], g4_r.at[0], ctx=sib).wait_recv()
+    d_total = jnp.concatenate([gfin[0], gfin[1]], axis=1)
+    nf = neg_ref[...].astype(F32)
+    scale = lax.rsqrt(jnp.sum(nf * nf, axis=1, keepdims=True) + 1e-06)
+    unit = nf * scale
+    dneg_ref[...] = scale * (d_total - unit * jnp.sum(unit * d_total, axis=1, keepdims=True))
 
     for d in near_first:
         yy = yo(d)
@@ -480,22 +564,16 @@
         dpre[:, cols] = (jnp.where(lo, even, swap(odd)) * slope(pre[:, cols])).astype(BF16)
         cols = slice(D + 128 * j, D + 128 * (j + 1))
         dpre[:, cols] = (jnp.where(lo, swap(even), odd) * slope(pre[:, cols])).astype(BF16)
-    dseq_ref[0] = (dout[...] + dot_nt(dpre[...], w_in_ref[...])).astype(BF16)
-
-    copy(gfin.at[1 - c], gfin.at[1 - c], g4_s.at[0], g4_r.at[0], ctx=sib).wait_recv()
-    d_total = jnp.concatenate([gfin[0], gfin[1]], axis=1)
-    nf = neg_ref[...].astype(F32)
-    scale = lax.rsqrt(jnp.sum(nf * nf, axis=1, keepdims=True) + 1e-06)
-    unit = nf * scale
-    dneg_ref[...] = scale * (d_total - unit * jnp.sum(unit * d_total, axis=1, keepdims=True))
+    d_seq = dout[...] + dot_nt(dpre[:, D : 2 * D], w_in_ref[:, D : 2 * D])
+    dseq_ref[0] = (d_seq + dot_nt(dpre[:, 3 * D :], w_in_ref[:, 3 * D :])).astype(BF16)
 
     for d in range(1, NY):
         kv_copy(d).wait_send()
         q_copy(d).wait_send()
-        mix_copy(d).wait_send()
+        mix_copy(yo(d)).wait_send()
         dm_copy(d).wait_send()
-        retq_copy(d).wait_send()
-        ret_copy(d).wait_send()
+        retq_copy(yo(d)).wait_send()
+        ret_copy(yo(d)).wait_send()
     for i in range(NY):
         relay(i).wait_send()
         sib_own(i).wait_send()
@@ -515,8 +593,7 @@
     @pl.when(x == 1)
     def _():
         for i in range(NY):
-            r = at(0, i, c)
-            copy(kv.at[r], kv.at[r], xr_s.at[i], xr_r.at[i], ctx=sib).wait_send()
+            cross_relay(i, c).wait_send()
             sib_cross(i).wait_send()
             cross(i).wait_send()
 
@@ -532,7 +609,6 @@
 
     def shards(seq_in, w_in, w_out, pos_emb, pos_ids, neg_emb, neg_ids, neg_counts):
         vm = pl.BlockSpec(memory_space=pltpu.VMEM)
-        sm = pl.BlockSpec(memory_space=pltpu.SMEM)
         return pl.pallas_call(
             body,
             out_shape=(
@@ -540,9 +616,18 @@
                 jax.ShapeDtypeStruct((1, ROWS, D), BF16),
                 jax.ShapeDtypeStruct((8, D), F32),
             ),
-            in_specs=[vm] * 6 + [sm] * 2,
+            in_specs=[pl.BlockSpec(memory_space=pltpu.HBM)] * 8,
             out_specs=(vm, vm, vm),
             scratch_shapes=[
+                V((1, ROWS, D), BF16),
+                V((D, 4 * D), BF16),
+                V((D, D), BF16),
+                V((1, ROWS, D), BF16),
+                V((1, ROWS), I32),
+                V((8, D), BF16),
+                pltpu.SMEM((8,), I32),
+                pltpu.SMEM((8,), I32),
+                S((9,)),
                 V((ROWS, 4 * D), F32),
                 V((NY, 128, 128), BF16),
                 V((NY, 64, 128), BF16),
@@ -555,7 +640,7 @@
                 V((NY, 64, 128), BF16),
                 V((NY, 64, 128), BF16),
                 V((NY * 128, 128), BF16),
-                V((NY // 2, 128, 256), BF16),
+                V((128, NY * 128), BF16),
                 V((NY * 128, 128), F32),
                 V((4 * NY, 128, 128), F32),
                 V((NY, 128, 128), F32),
@@ -584,7 +669,7 @@
             + [S((2 * NY,))] * 2
             + [S((1,))] * 2,
             compiler_params=pltpu.CompilerParams(
-                collective_id=0, has_side_effects=True, vmem_limit_bytes=48 << 20
+                collective_id=0, has_side_effects=True, vmem_limit_bytes=60 << 20
             ),
         )(seq_in, w_in, w_out, pos_emb, pos_ids, neg_emb, neg_ids, neg_counts)
 

time: 96.4 us -> 79.6 us (0.83)
  Pallas kernels: 86.6 us -> 74.7 us
  local copies, waits for them, and re-layouts: 8.87 us -> 4.05 us
    pallas_call x1, Pallas kernels: 86.6 us -> 74.7 us  [shards(): pl.pallas_call(body, out_shape=(jax.ShapeDtypeStruct((1, ROWS), F32), jax...]
    unnamed x19 -> x3, local copies, waits for them, and re-layouts: 8.87 us -> 4.05 us
where the time goes in v2:
time: 79.6 us; the launch traced here: 79.4 us
  Pallas kernels  74.7 us (94%)
  local copies, waits for them, and re-layouts  4.05 us (5%)
    pallas_call x1, Pallas kernels, shards(): pl.pallas_call(body, out_shape=(jax.ShapeDtypeStruct((1, ROWS), F32), jax...  74.7 us
    unnamed x3, local copies, waits for them, and re-layouts  4.05 us

profile of v2, /device:TPU:1, one launch (start us, length us, event | category | flops | bytes accessed | tf_op | source)
XLA Modules:
  0.0 79.4 jit_solution(2792643713228519118)
XLA Ops:
  0.6 74.7 %shard_map.103 = (f32[1,128]{1,0:T(1,128)}, bf16[1,128,512]{2,1,0:T(8,128)(2,1)}, f32[8,512]{1,0:T(8,128)}) custom-call(bf16[1,128,512]{2,1,0:T(8,128)(2,1)} %refs_0_.1, bf16[512,2048]{1,0:T(8,128)(2,1)} %refs_1_.1, bf16[512,512]{1,0:T(8,128)(2,1)} %refs_2_.1, bf16[1,128,512]{2,1,0:T(8,128)(2,1)} %refs_3_.1, s32[1,128]{1,0:T(1,128)} %refs_4_.1, ...), custom_call_target="tpu_custom_call" | custom-call | tf_op jit(solution)/shard_map/pallas_call | solution.py:612
  75.3 1.2 %copy.14 = f32[1,128]{1,0:T(1,128)} copy(f32[1,128]{1,0:T(1,128)} %get-tuple-element.6) | data formatting | bytes 1024
  76.5 1.6 %copy.15 = bf16[1,128,512]{2,1,0:T(8,128)(2,1)} copy(bf16[1,128,512]{2,1,0:T(8,128)(2,1)} %get-tuple-element.7) | data formatting | bytes 262144
  78.1 1.3 %copy.16 = f32[8,512]{1,0:T(8,128)} copy(f32[8,512]{1,0:T(8,128)} %get-tuple-element.8) | data formatting | bytes 32768

commit v3 on v2

--- a/solution.py
+++ b/solution.py
@@ -52,10 +52,10 @@
     loss_ref, dseq_ref, dneg_ref,
     seq_ref, w_in_ref, w_out_ref, pos_ref, pid_ref, neg_ref, nid_ref, ncnt_ref, in_s,
     pre, skv, sq, kv, rq, qz, acc, smix, rmix, sdm, rdm, dmz, qdt, dq, dkv,
-    sibo, sibx, sx, rx, sret, rret, sretq, rretq, dout, dpre, negs, nega, gsend, grecv, g1, g2, g3, g4, gfin,
+    sibo, sibx, sx, rx, sxq, rxq, smx, rmx, sret, rret, sretq, rretq, dout, dpre, negs, nega, gsend, grecv, g1, g2, g3, g4, gfin,
     kv_s, kv_r, q_s, q_r, rel_s, rel_r, xf_s, xf_r, xr_s, xr_r, mix_s, mix_r, dm_s, dm_r,
-    so_s, so_r, sx_s, sx_r, xx_s, xx_r, ret_s, ret_r, retq_s, retq_r,
-    neg_s, neg_r, gb_s, gb_r, g1_s, g1_r, gc_s, gc_r, g4_s, g4_r,
+    qf_s, qf_r, mx_s, mx_r, df_s, df_r, xq_s, xq_r, so_s, so_r, sx_s, sx_r, xx_s, xx_r, ret_s, ret_r, retq_s, retq_r,
+    neg_s, neg_r, gb_s, gb_r, g1_s, g1_r, gc_s, gc_r, g4_s, g4_r, hello,
 ):
     D = HEAD * NY
     T = NY // 2
@@ -107,7 +107,11 @@
     for p in [sib] + others + across:
         pl.semaphore_signal(barrier, inc=1, device_id={"ctx": p}, device_id_type=MESH)
     for d in range(1, NB):
-        pl.semaphore_signal(barrier, inc=1, device_id={"batch": bo(d)}, device_id_type=MESH)
+
+        @pl.when(bo(d) > b)
+        def _():
+            pl.semaphore_signal(barrier, inc=1, device_id={"batch": bo(d)}, device_id_type=MESH)
+
 
     loads[0].wait()
     loads[1].wait()
@@ -143,7 +147,7 @@
         )
     negs[:, D:] = meta
 
-    pl.semaphore_wait(barrier, 1 + (NY - 1) + NY + (NB - 1))
+    pl.semaphore_wait(barrier, 1 + (NY - 1) + NY + b)
 
     def kv_copy(d):
         h = yo(d)
@@ -167,24 +171,35 @@
     def own_relay():
         return copy(skv.at[y], kv.at[me], rel_s.at[y], rel_r.at[y], ctx=sib)
 
+    E = NY // 2
+
     def forward(yy):
         r = at(0, yy, c)
-        return copy(kv.at[r], kv.at[r], xf_s.at[yy], xf_r.at[yy], ctx=at(1, y, c))
-
-    def own_forward():
-        return copy(skv.at[y], kv.at[me], xf_s.at[y], xf_r.at[y], ctx=at(1, y, c))
+        return copy(kv.at[r], kv.at[r], xf_s.at[yy], xf_r.at[yy], ctx=at(1 - x, y, c))
+
+    def q_forward(i):
+        return copy(rq.at[i], rq.at[NY + i], qf_s.at[i], qf_r.at[i], ctx=at(1 - x, y, c))
 
     own_relay().start()
 
-    @pl.when(x == 0)
-    def _():
-        own_forward().start()
+    @pl.when(jnp.logical_and(x == 0, y >= E))
+    def _():
+        copy(skv.at[y], kv.at[me], xf_s.at[y], xf_r.at[y], ctx=at(1 - x, y, c)).start()
+
+    @pl.when(x == 1)
+    def _():
+        copy(sq.at[y], rq.at[NY + y], qf_s.at[y], qf_r.at[y], ctx=at(1 - x, y, c)).start()
 
     def neg_copy(d):
         return copy(negs, nega.at[b], neg_s.at[d], neg_r.at[b], batch=bo(d))
 
     for d in range(1, NB):
-        neg_copy(d).start()
+
+        @pl.when(bo(d) < b)
+        def _():
+            pl.semaphore_signal(hello, inc=1, device_id={"batch": bo(d)}, device_id_type=MESH)
+            neg_copy(d).start()
+
     nega[b] = negs[...]
 
     g_pre = dot_nn(xin, w_in_ref[:, :D])
@@ -196,18 +211,36 @@
         copy(skv.at[yy], kv.at[at(x, yy, c)], kv_s.at[yy], kv_r.at[yy], ctx=at(x, yy, c)).wait_recv()
         relay(yy).start()
 
-        @pl.when(x == 0)
+        @pl.when(jnp.logical_and(x == 0, yy >= E))
         def _():
             forward(yy).start()
 
-    for d in near_first:
-        yy = yo(d)
         copy(sq.at[yy], rq.at[yy], q_s.at[yy], q_r.at[yy], ctx=at(x, yy, c)).wait_recv()
+
+        @pl.when(x == 1)
+        def _():
+            q_forward(yy).start()
+
     half = low((64, 128))
-    for i in range(NY):
+
+    @pl.when(b < NB - 1)
+    def _():
+        pl.semaphore_wait(hello, NB - 1 - b)
+
+    for d in range(1, NB):
+
+        @pl.when(bo(d) > b)
+        def _():
+            neg_copy(d).start()
+
+
+    def take_q(i):
         v = rq[i].astype(F32)
         qz[i * 128 : i * 128 + 64] = jnp.where(half, v, 0.0).astype(BF16)
         qz[i * 128 + 64 : i * 128 + 128] = jnp.where(half, swap(v), 0.0).astype(BF16)
+
+    for i in range(NY):
+        take_q(i)
     for d in range(NY):
         yy = yo(d)
         r = at(x, yy, 1 - c)
@@ -232,19 +265,23 @@
     def mix_copy(i):
         return copy(smix.at[i], rmix.at[y], mix_s.at[i], mix_r.at[y], ctx=at(x, i, c))
 
-    def send_mixed(k, rows):
-        for e in range(2):
-            i = 2 * k + e
-            top, bottom = rows[e * 128 : e * 128 + 64], rows[e * 128 + 64 : e * 128 + 128]
-            smix[i] = jnp.where(half, swap(top), bottom).astype(BF16)
-
-            @pl.when(y == i)
-            def _():
-                rmix[y] = smix[i]
-
-            @pl.when(y != i)
-            def _():
-                mix_copy(i).start()
+    def pack_mixed(rows, e):
+        top, bottom = rows[e * 128 : e * 128 + 64], rows[e * 128 + 64 : e * 128 + 128]
+        return jnp.where(half, swap(top), bottom)
+
+    def send_mixed(i, packed):
+        smix[i] = packed.astype(BF16)
+
+        @pl.when(y == i)
+        def _():
+            rmix[y] = smix[i]
+
+        @pl.when(y != i)
+        def _():
+            mix_copy(i).start()
+
+    def mix_cross(i):
+        return copy(smx.at[i], rmx.at[i], mx_s.at[i], mx_r.at[i], ctx=at(1 - x, y, c))
 
     def cross_in(yy):
         r = at(0, yy, c)
@@ -254,38 +291,52 @@
         r = at(0, yy, cc)
         return copy(kv.at[r], kv.at[r], xr_s.at[yy], xr_r.at[yy], ctx=sib)
 
-    def take_cross(ds):
-        @pl.when(x == 1)
-        def _():
-            for d in ds:
-                cross_in(yo(d)).wait_recv()
-                cross_relay(yo(d), c).start()
-
-    order = [0] + near_first
-    take_cross(order[: NY // 2])
     for k in range(T):
         if k == T - 1:
-            take_cross(order[NY // 2 :])
+
+            @pl.when(x == 1)
+            def _():
+                for i in range(E, NY):
+                    cross_in(i).wait_recv()
+                    cross_relay(i, c).start()
+
         tile = kv[pl.ds(x * 2 * NY, 4 * (k + 1))].reshape(512 * (k + 1), 128)
         rows = weighted(qz[256 * k : 256 * (k + 1)], tile, True)
 
         @pl.when(x == 0)
         def _():
-            send_mixed(k, rows)
+            for e in range(2):
+                send_mixed(2 * k + e, pack_mixed(rows, e))
 
         @pl.when(x == 1)
         def _():
             acc[256 * k : 256 * (k + 1)] = rows
 
+    W = 128 * T
+
+    @pl.when(x == 0)
+    def _():
+        for i in range(NY):
+            q_forward(i).wait_recv()
+            take_q(NY + i)
+        tile = kv[:NY].reshape(128 * NY, 128)
+        for n in range(2):
+            rows = weighted(qz[256 * T + W * n : 256 * T + W * (n + 1)], tile, False)
+            for e in range(T):
+                smx[n * T + e] = pack_mixed(rows, e).astype(BF16)
+                mix_cross(n * T + e).start()
 
     @pl.when(x == 1)
     def _():
-        for d in order:
-            cross_relay(yo(d), 1 - c).wait_recv()
-        tile = kv[: 2 * NY].reshape(512 * T, 128)
-        for k in range(T):
-            rows = slice(256 * k, 256 * (k + 1))
-            send_mixed(k, acc[rows] + weighted(qz[rows], tile, False))
+        for i in range(E, NY):
+            cross_relay(i, 1 - c).wait_recv()
+        tile = kv[NY : 2 * NY].reshape(128 * NY, 128)
+        for n in range(2):
+            piece = slice(W * n, W * (n + 1))
+            acc[piece] += weighted(qz[piece], tile, False)
+        for i in range(NY):
+            mix_cross(i).wait_recv()
+            send_mixed(i, pack_mixed(acc[i * 128 : (i + 1) * 128], 0) + rmx[i].astype(F32))
 
     for d in range(1, NB):
         bb = bo(d)
@@ -355,7 +406,9 @@
     dout[...] = d_out + dot_nt(d_pre, w_in_ref[:, :D])
     loss_ref[...] = jnp.transpose(jnp.broadcast_to(loss, (ROWS, 128)))[0:1, :]
     grad = dot_nn(jnp.transpose(probs).astype(BF16), user_b) * TEMPER_INV
-    gsend[...] = grad.reshape(NB, 8, D)
+    for j in range(D // 256):
+        pair = [grad[:, 256 * j + 128 * e : 256 * j + 128 * (e + 1)].reshape(NB, 8, 128) for e in range(2)]
+        gsend[:, 16 * j : 16 * (j + 1), :] = jnp.concatenate(pair, axis=1).astype(BF16)
 
     def gb_copy(d):
         bb = bo(d)
@@ -366,16 +419,30 @@
     grecv[b] = gsend[b]
     dq[...] = jnp.zeros_like(dq)
 
+    def dm_forward(i):
+        return copy(rdm.at[i], rdm.at[NY + i], df_s.at[i], df_r.at[i], ctx=at(1 - x, y, c))
+
+    def pass_dm(i):
+        @pl.when(x == 1)
+        def _():
+            dm_forward(i).start()
+
+    pass_dm(y)
     for d in near_first:
         yy = yo(d)
         copy(sdm.at[yy], rdm.at[yy], dm_s.at[yy], dm_r.at[yy], ctx=at(x, yy, c)).wait_recv()
-    for i in range(NY):
+        pass_dm(yy)
+
+    def take_dm(i):
         v = rdm[i].astype(F32)
         up = jnp.concatenate([jnp.where(half, 0.0, swap(v)), jnp.where(half, 0.0, v)], axis=0)
         dmz[i * 128 : i * 128 + 128] = up.astype(BF16)
         both = up + qz[i * 128 : i * 128 + 128].astype(F32)
         qdt[:, i * 128 : i * 128 + 128] = jnp.transpose(both).astype(BF16)
 
+    for i in range(NY):
+        take_dm(i)
+
     def g1_copy():
         return copy(g1, g2, g1_s.at[0], g1_r.at[0], ctx=sib)
 
@@ -389,19 +456,19 @@
         return copy(gfin.at[c], gfin.at[c], g4_s.at[0], g4_r.at[0], ctx=sib)
 
     peers = [(d, 0) for d in range(1, NY)] + [(d, 1) for d in range(NY)]
-    H = D // 2
+    H = D // 32
 
     def g_histories():
         for d in range(1, NB):
             bb = bo(d)
             copy(gsend.at[bb], grecv.at[bb], gb_s.at[d], gb_r.at[bb], batch=bb).wait_recv()
-        g1[...] = jnp.sum(grecv[...], axis=0)
+        g1[...] = jnp.sum(grecv[...].astype(F32), axis=0)
         g1_copy().start()
 
     def g_pair():
         g1_copy().wait_recv()
         gsum = g1[...] + g2[...]
-        g3[...] = jnp.where(c == 0, gsum[:, :H], gsum[:, H:])
+        g3[...] = jnp.where(c == 0, gsum[:H], gsum[H:]).astype(BF16)
         for d, xx in peers:
             gc_copy(d, xx).start()
         g4[x * NY + y] = g3[...]
@@ -410,12 +477,11 @@
         for d, xx in peers:
             s = (x if xx == 0 else 1 - x) * NY + yo(d)
             copy(g3, g4.at[s], gc_s.at[xx * NY + d], gc_r.at[s], ctx=sib).wait_recv()
-        gfin[c] = jnp.sum(g4[...], axis=0)
+        gfin[c] = jnp.sum(g4[...].astype(F32), axis=0)
         g4_copy().start()
 
-    def bwd(k0, t, diagonal):
-        rows = slice(256 * k0, 256 * T)
-        tile = keys_of(t)
+    def bwd(rows, block, blocks, diagonal, more):
+        tile = kv[pl.ds(block, blocks)].reshape(128 * blocks, 128)
         h = dot_nt(qz[rows], tile)
         dw = dot_nt(dmz[rows], tile)
         th = jnp.tanh(h)
@@ -435,9 +501,14 @@
         dq[rows] += dot_nn(ds, tile)
         dk = dot_nn(qdt[:64, rows], ds)
         dv = dot_nn(qdt[64:, rows], w)
-        for j in range(4):
-            dkv[t * 4 + j, :64, :] = dk[:, 128 * j : 128 * (j + 1)]
-            dkv[t * 4 + j, 64:, :] = dv[:, 128 * j : 128 * (j + 1)]
+        for j in range(blocks):
+            one = slice(128 * j, 128 * (j + 1))
+            if more:
+                dkv[block + j, :64, :] += dk[:, one]
+                dkv[block + j, 64:, :] += dv[:, one]
+            else:
+                dkv[block + j, :64, :] = dk[:, one]
+                dkv[block + j, 64:, :] = dv[:, one]
 
     def sib_own(yy):
         return copy(dkv.at[at(x, yy, 1 - c)], sibo.at[yy], so_s.at[yy], so_r.at[yy], ctx=sib)
@@ -461,11 +532,18 @@
     def ret_copy(i):
         return copy(sret.at[i], rret.at[y], ret_s.at[i], ret_r.at[y], ctx=at(x, i, c))
 
-    def send_dq(k):
+    def pack_dq(i):
+        top = dq[i * 128 : i * 128 + 64] * 0.0625
+        bottom = dq[i * 128 + 64 : i * 128 + 128] * 0.0625
+        return jnp.where(half, top, swap(bottom))
+
+    def send_dq(k, crossed):
         for i in (2 * k, 2 * k + 1):
-            top = dq[i * 128 : i * 128 + 64] * 0.0625
-            bottom = dq[i * 128 + 64 : i * 128 + 128] * 0.0625
-            sretq[i] = jnp.where(half, top, swap(bottom)).astype(BF16)
+            mine = pack_dq(i)
+            if crossed:
+                dq_cross(i).wait_recv()
+                mine = mine + rxq[i].astype(F32)
+            sretq[i] = mine.astype(BF16)
 
             @pl.when(y == i)
             def _():
@@ -474,6 +552,9 @@
             @pl.when(y != i)
             def _():
                 retq_copy(i).start()
+
+    def dq_cross(i):
+        return copy(sxq.at[i], rxq.at[i], xq_s.at[i], xq_r.at[i], ctx=at(1 - x, y, c))
 
     def send_dkv(t, crossed):
         for i in (2 * t, 2 * t + 1):
@@ -493,67 +574,85 @@
                 ret_copy(i).start()
 
 
+    HALF = T // 2
+    every = slice(0, 256 * T)
+
     @pl.when(x == 1)
     def _():
-        @pl.loop(0, T)
-        def _(t):
-            bwd(0, t, False)
+        for t in range(HALF, T):
+            bwd(every, 4 * t, 4, False, False)
             for e in range(2):
                 sib_cross(2 * t + e).start()
-
-            @pl.when(t > 0)
-            def _():
+            if t > HALF:
                 cross_sums(t - 1)
 
-    steps = [T - 1] + list(range(T - 1))
-    for n, t in enumerate(steps):
-        bwd(t, x * T + t, True)
-        for i in (2 * t, 2 * t + 1):
+    for t in range(T):
+        bwd(slice(256 * t, 256 * T), (x * T + t) * 4, 4, True, False)
+
+        @pl.when(jnp.logical_or(x == 1, t >= HALF))
+        def _():
+            for e in range(2):
+                sib_own(2 * t + e).start()
+
+        @pl.when(x == 1)
+        def _():
+            if t == 0:
+                cross_sums(T - 1)
+            else:
+                send_dkv(t - 1, False)
+
+        @pl.when(x == 0)
+        def _():
+            send_dq(t, False)
+
+    g_histories()
+
+
+    @pl.when(x == 0)
+    def _():
+        for i in range(NY):
+            dm_forward(i).wait_recv()
+            take_dm(NY + i)
+        for n in range(2):
+            bwd(slice(256 * T + 128 * T * n, 256 * T + 128 * T * (n + 1)), 0, 4 * HALF, False, True)
+            for e in range(T):
+                i = n * T + e
+                sxq[i] = pack_dq(NY + i).astype(BF16)
+                dq_cross(i).start()
+        for i in range(2 * HALF):
             sib_own(i).start()
-        if n == 0:
-
-            @pl.when(x == 1)
-            def _():
-                cross_sums(T - 1)
-
-            g_histories()
-        else:
-            send_dq(t)
-
-            @pl.when(x == 1)
-            def _():
-                send_dkv(steps[n - 1], False)
-        if n == 1 or T == 1:
-            g_pair()
-    send_dq(T - 1)
 
 
     @pl.when(x == 1)
     def _():
-        send_dkv(steps[-1], False)
+        send_dkv(T - 1, False)
+
+    g_pair()
+
+    @pl.when(x == 1)
+    def _():
+        for k in range(T):
+            send_dq(k, True)
 
     @pl.when(x == 0)
     def _():
-        for t in range(T):
-            send_dkv(t, True)
-
-    g_chips()
-
-    for d in near_first:
-        yy = yo(d)
-        copy(sretq.at[yy], rretq.at[yy], retq_s.at[yy], retq_r.at[yy], ctx=at(x, yy, c)).wait_recv()
-    for j in range(NY // 2):
-        cols = slice(2 * D + 128 * j, 2 * D + 128 * (j + 1))
-        d_q = unpack_pair(rretq[2 * j].astype(F32), rretq[2 * j + 1].astype(F32))
-        dpre[:, cols] = (d_q * slope(pre[:, cols])).astype(BF16)
-    dout[...] += dot_nt(dpre[:, 2 * D : 3 * D], w_in_ref[:, 2 * D : 3 * D])
-
-    copy(gfin.at[1 - c], gfin.at[1 - c], g4_s.at[0], g4_r.at[0], ctx=sib).wait_recv()
-    d_total = jnp.concatenate([gfin[0], gfin[1]], axis=1)
-    nf = neg_ref[...].astype(F32)
-    scale = lax.rsqrt(jnp.sum(nf * nf, axis=1, keepdims=True) + 1e-06)
-    unit = nf * scale
-    dneg_ref[...] = scale * (d_total - unit * jnp.sum(unit * d_total, axis=1, keepdims=True))
+        for t in list(range(HALF, T)) + list(range(HALF)):
+            send_dkv(t, t >= HALF)
+
+    def finish_dq():
+        for d in near_first:
+            yy = yo(d)
+            copy(sretq.at[yy], rretq.at[yy], retq_s.at[yy], retq_r.at[yy], ctx=at(x, yy, c)).wait_recv()
+        for j in range(NY // 2):
+            cols = slice(2 * D + 128 * j, 2 * D + 128 * (j + 1))
+            d_q = unpack_pair(rretq[2 * j].astype(F32), rretq[2 * j + 1].astype(F32))
+            dpre[:, cols] = (d_q * slope(pre[:, cols])).astype(BF16)
+        dout[...] += dot_nt(dpre[:, 2 * D : 3 * D], w_in_ref[:, 2 * D : 3 * D])
+
+
+    @pl.when(x == 0)
+    def _():
+        finish_dq()
 
     for d in near_first:
         yy = yo(d)
@@ -564,8 +663,21 @@
         dpre[:, cols] = (jnp.where(lo, even, swap(odd)) * slope(pre[:, cols])).astype(BF16)
         cols = slice(D + 128 * j, D + 128 * (j + 1))
         dpre[:, cols] = (jnp.where(lo, swap(even), odd) * slope(pre[:, cols])).astype(BF16)
-    d_seq = dout[...] + dot_nt(dpre[:, D : 2 * D], w_in_ref[:, D : 2 * D])
-    dseq_ref[0] = (d_seq + dot_nt(dpre[:, 3 * D :], w_in_ref[:, 3 * D :])).astype(BF16)
+    dout[...] += dot_nt(dpre[:, D : 2 * D], w_in_ref[:, D : 2 * D]) + dot_nt(dpre[:, 3 * D :], w_in_ref[:, 3 * D :])
+    g_chips()
+
+    @pl.when(x == 1)
+    def _():
+        finish_dq()
+
+    dseq_ref[0] = dout[...].astype(BF16)
+
+    copy(gfin.at[1 - c], gfin.at[1 - c], g4_s.at[0], g4_r.at[0], ctx=sib).wait_recv()
+    d_total = jnp.concatenate([gfin[e // (H // 8), 8 * (e % (H // 8)) : 8 * (e % (H // 8)) + 8] for e in range(D // 128)], axis=1)
+    nf = neg_ref[...].astype(F32)
+    scale = lax.rsqrt(jnp.sum(nf * nf, axis=1, keepdims=True) + 1e-06)
+    unit = nf * scale
+    dneg_ref[...] = scale * (d_total - unit * jnp.sum(unit * d_total, axis=1, keepdims=True))
 
     for d in range(1, NY):
         kv_copy(d).wait_send()
@@ -588,14 +700,20 @@
     @pl.when(x == 0)
     def _():
         for i in range(NY):
+            mix_cross(i).wait_send()
+            dq_cross(i).wait_send()
+        for i in range(E, NY):
             forward(i).wait_send()
 
     @pl.when(x == 1)
     def _():
         for i in range(NY):
-            cross_relay(i, c).wait_send()
+            q_forward(i).wait_send()
+            dm_forward(i).wait_send()
+        for i in range(2 * HALF, NY):
             sib_cross(i).wait_send()
             cross(i).wait_send()
+            cross_relay(i, c).wait_send()
 
 
 def solution(mesh):
@@ -632,21 +750,25 @@
                 V((NY, 128, 128), BF16),
                 V((NY, 64, 128), BF16),
                 V((4 * NY, 128, 128), BF16),
-                V((NY, 64, 128), BF16),
-                V((NY * 128, 128), BF16),
+                V((2 * NY, 64, 128), BF16),
+                V((NY * 256, 128), BF16),
                 V((NY * 128, 128), F32),
                 V((NY, 64, 128), BF16),
                 V((NY, 64, 128), BF16),
                 V((NY, 64, 128), BF16),
-                V((NY, 64, 128), BF16),
-                V((NY * 128, 128), BF16),
-                V((128, NY * 128), BF16),
-                V((NY * 128, 128), F32),
+                V((2 * NY, 64, 128), BF16),
+                V((NY * 256, 128), BF16),
+                V((128, NY * 256), BF16),
+                V((NY * 256, 128), F32),
                 V((4 * NY, 128, 128), F32),
                 V((NY, 128, 128), F32),
                 V((NY, 128, 128), F32),
                 V((NY, 128, 128), BF16),
                 V((NY, 128, 128), BF16),
+                V((NY, 64, 128), BF16),
+                V((NY, 64, 128), BF16),
+                V((NY, 64, 128), BF16),
+                V((NY, 64, 128), BF16),
                 V((NY, 128, 128), BF16),
                 V((NY, 128, 128), BF16),
                 V((NY, 64, 128), BF16),
@@ -655,19 +777,20 @@
                 V((ROWS, 4 * D), BF16),
                 V((8, D + 128), F32),
                 V((NB, 8, D + 128), F32),
-                V((NB, 8, D), F32),
-                V((NB, 8, D), F32),
-                V((8, D), F32),
-                V((8, D), F32),
-                V((8, D // 2), F32),
-                V((2 * NY, 8, D // 2), F32),
-                V((2, 8, D // 2), F32),
+                V((NB, D // 16, 128), BF16),
+                V((NB, D // 16, 128), BF16),
+                V((D // 16, 128), F32),
+                V((D // 16, 128), F32),
+                V((D // 32, 128), BF16),
+                V((2 * NY, D // 32, 128), BF16),
+                V((2, D // 32, 128), F32),
             ]
-            + [S((NY,))] * 24
+            + [S((NY,))] * 32
             + [S((NB,))] * 4
             + [S((1,))] * 2
             + [S((2 * NY,))] * 2
-            + [S((1,))] * 2,
+            + [S((1,))] * 2
+            + [pltpu.SemaphoreType.REGULAR],
             compiler_params=pltpu.CompilerParams(
                 collective_id=0, has_side_effects=True, vmem_limit_bytes=60 << 20
             ),

time: 79.6 us -> 72.3 us (0.908)
  Pallas kernels: 74.7 us -> 67.4 us
    pallas_call x1, Pallas kernels: 74.7 us -> 67.4 us  [shards(): pl.pallas_call(body, out_shape=(jax.ShapeDtypeStruct((1, ROWS), F32), jax...]
where the time goes in v3:
time: 72.3 us; the launch traced here: 72 us
  Pallas kernels  67.4 us (93%)
  local copies, waits for them, and re-layouts  4.05 us (6%)
    pallas_call x1, Pallas kernels, shards(): pl.pallas_call(body, out_shape=(jax.ShapeDtypeStruct((1, ROWS), F32), jax...  67.4 us
    unnamed x3, local copies, waits for them, and re-layouts  4.05 us

profile of v3, /device:TPU:1, one launch (start us, length us, event | category | flops | bytes accessed | tf_op | source)
XLA Modules:
  0.0 72.0 jit_solution(12189640619557575951)
XLA Ops:
  0.6 67.4 %shard_map.103 = (f32[1,128]{1,0:T(1,128)}, bf16[1,128,512]{2,1,0:T(8,128)(2,1)}, f32[8,512]{1,0:T(8,128)}) custom-call(bf16[1,128,512]{2,1,0:T(8,128)(2,1)} %refs_0_.1, bf16[512,2048]{1,0:T(8,128)(2,1)} %refs_1_.1, bf16[512,512]{1,0:T(8,128)(2,1)} %refs_2_.1, bf16[1,128,512]{2,1,0:T(8,128)(2,1)} %refs_3_.1, s32[1,128]{1,0:T(1,128)} %refs_4_.1, ...), custom_call_target="tpu_custom_call" | custom-call | tf_op jit(solution)/shard_map/pallas_call | solution.py:730
  68.0 1.2 %copy.14 = f32[1,128]{1,0:T(1,128)} copy(f32[1,128]{1,0:T(1,128)} %get-tuple-element.6) | data formatting | bytes 1024
  69.2 1.6 %copy.15 = bf16[1,128,512]{2,1,0:T(8,128)(2,1)} copy(bf16[1,128,512]{2,1,0:T(8,128)(2,1)} %get-tuple-element.7) | data formatting | bytes 262144
  70.7 1.3 %copy.16 = f32[8,512]{1,0:T(8,128)} copy(f32[8,512]{1,0:T(8,128)} %get-tuple-element.8) | data formatting | bytes 32768

commit v4 on v3

--- a/solution.py
+++ b/solution.py
@@ -52,10 +52,10 @@
     loss_ref, dseq_ref, dneg_ref,
     seq_ref, w_in_ref, w_out_ref, pos_ref, pid_ref, neg_ref, nid_ref, ncnt_ref, in_s,
     pre, skv, sq, kv, rq, qz, acc, smix, rmix, sdm, rdm, dmz, qdt, dq, dkv,
-    sibo, sibx, sx, rx, sxq, rxq, smx, rmx, sret, rret, sretq, rretq, dout, dpre, negs, nega, gsend, grecv, g1, g2, g3, g4, gfin,
+    sibo, sibx, sx, rx, sxq, rxq, smx, rmx, sret, rret, sretq, rretq, dout, dpre, negs, nega, gsend, grecv, g1, g2, g3, g3x, gsum, g4, gfin,
     kv_s, kv_r, q_s, q_r, rel_s, rel_r, xf_s, xf_r, xr_s, xr_r, mix_s, mix_r, dm_s, dm_r,
     qf_s, qf_r, mx_s, mx_r, df_s, df_r, xq_s, xq_r, so_s, so_r, sx_s, sx_r, xx_s, xx_r, ret_s, ret_r, retq_s, retq_r,
-    neg_s, neg_r, gb_s, gb_r, g1_s, g1_r, gc_s, gc_r, g4_s, g4_r, hello,
+    neg_s, neg_r, gb_s, gb_r, g1_s, g1_r, gc_s, gc_r, g4_s, g4_r, gx_s, gx_r, hello,
 ):
     D = HEAD * NY
     T = NY // 2
@@ -76,7 +76,7 @@
 
     sib = at(x, y, 1 - c)
     others = [at(x, yo(d), c) for d in range(1, NY)]
-    across = [at(1 - x, yo(d), c) for d in range(NY)]
+    across = at(1 - x, y, c)
 
     def copy(src, dst, ss, rs, ctx=None, batch=None):
         where = {"ctx": ctx} if batch is None else {"batch": batch}
@@ -90,7 +90,10 @@
         for i, (src, dst) in enumerate(
             [
                 (seq_hbm, seq_ref),
-                (w_in_hbm.at[:, D:], w_in_ref.at[:, D:]),
+                *[
+                    (w_in_hbm.at[pl.ds(r * D // 4, D // 4), D:], w_in_ref.at[pl.ds(r * D // 4, D // 4), D:])
+                    for r in range(4)
+                ],
                 (w_in_hbm.at[:, :D], w_in_ref.at[:, :D]),
                 (neg_hbm, neg_ref),
                 (nid_hbm, nid_ref),
@@ -104,7 +107,7 @@
     for load in loads:
         load.start()
     barrier = pltpu.get_barrier_semaphore()
-    for p in [sib] + others + across:
+    for p in [sib, across] + others:
         pl.semaphore_signal(barrier, inc=1, device_id={"ctx": p}, device_id_type=MESH)
     for d in range(1, NB):
 
@@ -113,8 +116,8 @@
             pl.semaphore_signal(barrier, inc=1, device_id={"batch": bo(d)}, device_id_type=MESH)
 
 
-    loads[0].wait()
-    loads[1].wait()
+    for load in loads[:5]:
+        load.wait()
     xin = seq_ref[0]
     lane = lax.broadcasted_iota(I32, (ROWS, 128), 1)
     lo = lane < HEAD
@@ -133,7 +136,7 @@
         sq[2 * j] = pack_rows(qt, 0).astype(BF16)
         sq[2 * j + 1] = pack_rows(qt, 1).astype(BF16)
 
-    for load in loads[2:]:
+    for load in loads[5:]:
         load.wait()
     negs[:, :D] = neg_ref[...].astype(F32)
     meta_lane = lax.broadcasted_iota(I32, (8, 128), 1)
@@ -147,7 +150,7 @@
         )
     negs[:, D:] = meta
 
-    pl.semaphore_wait(barrier, 1 + (NY - 1) + NY + b)
+    pl.semaphore_wait(barrier, 2 + (NY - 1) + b)
 
     def kv_copy(d):
         h = yo(d)
@@ -158,9 +161,20 @@
         return copy(sq.at[h], rq.at[y], q_s.at[h], q_r.at[y], ctx=at(x, h, c))
 
     far_first = sorted(range(1, NY), key=lambda d: -min(d, NY - d))
-    for d in far_first:
-        kv_copy(d).start()
-        q_copy(d).start()
+    @pl.when(x == 0)
+    def _():
+        for d in far_first:
+            kv_copy(d).start()
+        for d in far_first:
+            q_copy(d).start()
+
+    @pl.when(x == 1)
+    def _():
+        for d in far_first:
+            q_copy(d).start()
+        for d in far_first:
+            kv_copy(d).start()
+
     kv[me] = skv[y]
     rq[y] = sq[y]
 
@@ -206,6 +220,53 @@
     pre[:, :D] = g_pre
 
     near_first = far_first[::-1]
+    half = low((64, 128))
+
+    def take_q(i):
+        v = rq[i].astype(F32)
+        qz[i * 128 : i * 128 + 64] = jnp.where(half, v, 0.0).astype(BF16)
+        qz[i * 128 + 64 : i * 128 + 128] = jnp.where(half, swap(v), 0.0).astype(BF16)
+
+    def take_own_q():
+        for d in near_first:
+            yy = yo(d)
+            copy(sq.at[yy], rq.at[yy], q_s.at[yy], q_r.at[yy], ctx=at(x, yy, c)).wait_recv()
+
+            @pl.when(x == 1)
+            def _():
+                q_forward(yy).start()
+
+        for i in range(NY):
+            take_q(i)
+
+    def weighted(q, tile):
+        h = dot_nt(q, tile)
+        return h + h * jnp.tanh(h)
+
+    def pack_mixed(rows, e):
+        top, bottom = rows[e * 128 : e * 128 + 64], rows[e * 128 + 64 : e * 128 + 128]
+        return jnp.where(half, swap(top), bottom)
+
+    def mix_cross(i):
+        return copy(smx.at[i], rmx.at[i], mx_s.at[i], mx_r.at[i], ctx=at(1 - x, y, c))
+
+    W = 128 * T
+
+    def meet_higher():
+        @pl.when(b < NB - 1)
+        def _():
+            pl.semaphore_wait(hello, NB - 1 - b)
+
+        for d in range(1, NB):
+
+            @pl.when(bo(d) > b)
+            def _():
+                neg_copy(d).start()
+
+    @pl.when(x == 1)
+    def _():
+        take_own_q()
+
     for d in near_first:
         yy = yo(d)
         copy(skv.at[yy], kv.at[at(x, yy, c)], kv_s.at[yy], kv_r.at[yy], ctx=at(x, yy, c)).wait_recv()
@@ -215,60 +276,50 @@
         def _():
             forward(yy).start()
 
-        copy(sq.at[yy], rq.at[yy], q_s.at[yy], q_r.at[yy], ctx=at(x, yy, c)).wait_recv()
-
-        @pl.when(x == 1)
-        def _():
-            q_forward(yy).start()
-
-    half = low((64, 128))
-
-    @pl.when(b < NB - 1)
-    def _():
-        pl.semaphore_wait(hello, NB - 1 - b)
-
-    for d in range(1, NB):
-
-        @pl.when(bo(d) > b)
-        def _():
-            neg_copy(d).start()
-
-
-    def take_q(i):
-        v = rq[i].astype(F32)
-        qz[i * 128 : i * 128 + 64] = jnp.where(half, v, 0.0).astype(BF16)
-        qz[i * 128 + 64 : i * 128 + 128] = jnp.where(half, swap(v), 0.0).astype(BF16)
-
-    for i in range(NY):
-        take_q(i)
+
+    @pl.when(x == 1)
+    def _():
+        meet_higher()
+
     for d in range(NY):
         yy = yo(d)
         r = at(x, yy, 1 - c)
         copy(kv.at[r], kv.at[r], rel_s.at[yy], rel_r.at[yy], ctx=sib).wait_recv()
 
+
+    @pl.when(x == 0)
+    def _():
+        for i in range(NY):
+            q_forward(i).wait_recv()
+            take_q(NY + i)
+        tile = kv[:NY].reshape(128 * NY, 128)
+        for n in range(2):
+            w = weighted(qz[256 * T + W * n : 256 * T + W * (n + 1)], tile)
+            rows = dot_nn(w.astype(BF16), tile)
+            for e in range(T):
+                smx[n * T + e] = pack_mixed(rows, e).astype(BF16)
+                mix_cross(n * T + e).start()
+        meet_higher()
+        take_own_q()
+
     def keys_of(t):
         return kv[pl.ds(t * 4, 4)].reshape(512, 128)
 
-    def allowed():
-        i = lax.broadcasted_iota(I32, (256, 512), 0)
-        j = lax.broadcasted_iota(I32, (256, 512), 1)
-        return j <= i + jnp.where(i >= 128, 128, 0) + c * 128
-
-    def weighted(q, tile, diagonal):
-        h = dot_nt(q, tile)
-        w = h + h * jnp.tanh(h)
+    def allowed(rows, keys):
+        i = lax.broadcasted_iota(I32, (rows, keys), 0)
+        j = lax.broadcasted_iota(I32, (rows, keys), 1)
+        return j <= i + lax.shift_right_logical(i, 7) * 128 + c * 128
+
+    def rows_of(q, tile, diagonal):
+        w = weighted(q, tile)
         if diagonal:
-            last = jnp.where(allowed(), w[:, -512:], 0.0)
+            last = jnp.where(allowed(256, 512), w[:, -512:], 0.0)
             w = last if w.shape[1] == 512 else jnp.concatenate([w[:, :-512], last], axis=1)
         return dot_nn(w.astype(BF16), tile)
 
     def mix_copy(i):
         return copy(smix.at[i], rmix.at[y], mix_s.at[i], mix_r.at[y], ctx=at(x, i, c))
 
-    def pack_mixed(rows, e):
-        top, bottom = rows[e * 128 : e * 128 + 64], rows[e * 128 + 64 : e * 128 + 128]
-        return jnp.where(half, swap(top), bottom)
-
     def send_mixed(i, packed):
         smix[i] = packed.astype(BF16)
 
@@ -279,9 +330,6 @@
         @pl.when(y != i)
         def _():
             mix_copy(i).start()
-
-    def mix_cross(i):
-        return copy(smx.at[i], rmx.at[i], mx_s.at[i], mx_r.at[i], ctx=at(1 - x, y, c))
 
     def cross_in(yy):
         r = at(0, yy, c)
@@ -301,7 +349,7 @@
                     cross_relay(i, c).start()
 
         tile = kv[pl.ds(x * 2 * NY, 4 * (k + 1))].reshape(512 * (k + 1), 128)
-        rows = weighted(qz[256 * k : 256 * (k + 1)], tile, True)
+        rows = rows_of(qz[256 * k : 256 * (k + 1)], tile, True)
 
         @pl.when(x == 0)
         def _():
@@ -311,20 +359,6 @@
         @pl.when(x == 1)
         def _():
             acc[256 * k : 256 * (k + 1)] = rows
-
-    W = 128 * T
-
-    @pl.when(x == 0)
-    def _():
-        for i in range(NY):
-            q_forward(i).wait_recv()
-            take_q(NY + i)
-        tile = kv[:NY].reshape(128 * NY, 128)
-        for n in range(2):
-            rows = weighted(qz[256 * T + W * n : 256 * T + W * (n + 1)], tile, False)
-            for e in range(T):
-                smx[n * T + e] = pack_mixed(rows, e).astype(BF16)
-                mix_cross(n * T + e).start()
 
     @pl.when(x == 1)
     def _():
@@ -333,7 +367,7 @@
         tile = kv[NY : 2 * NY].reshape(128 * NY, 128)
         for n in range(2):
             piece = slice(W * n, W * (n + 1))
-            acc[piece] += weighted(qz[piece], tile, False)
+            acc[piece] += rows_of(qz[piece], tile, False)
         for i in range(NY):
             mix_cross(i).wait_recv()
             send_mixed(i, pack_mixed(acc[i * 128 : (i + 1) * 128], 0) + rmx[i].astype(F32))
@@ -446,16 +480,15 @@
     def g1_copy():
         return copy(g1, g2, g1_s.at[0], g1_r.at[0], ctx=sib)
 
-    def gc_copy(d, xx):
-        there = x if xx == 0 else 1 - x
-        return copy(
-            g3, g4.at[x * NY + y], gc_s.at[xx * NY + d], gc_r.at[x * NY + y], ctx=at(there, yo(d), c)
-        )
+    def gx_copy():
+        return copy(g3, g3x, gx_s.at[0], gx_r.at[0], ctx=across)
+
+    def gc_copy(d):
+        return copy(gsum, g4.at[y], gc_s.at[d], gc_r.at[y], ctx=at(x, yo(d), c))
 
     def g4_copy():
         return copy(gfin.at[c], gfin.at[c], g4_s.at[0], g4_r.at[0], ctx=sib)
 
-    peers = [(d, 0) for d in range(1, NY)] + [(d, 1) for d in range(NY)]
     H = D // 32
 
     def g_histories():
@@ -467,16 +500,20 @@
 
     def g_pair():
         g1_copy().wait_recv()
-        gsum = g1[...] + g2[...]
-        g3[...] = jnp.where(c == 0, gsum[:H], gsum[H:]).astype(BF16)
-        for d, xx in peers:
-            gc_copy(d, xx).start()
-        g4[x * NY + y] = g3[...]
+        total = g1[...] + g2[...]
+        g3[...] = jnp.where(c == 0, total[:H], total[H:])
+        gx_copy().start()
+
+    def g_across():
+        gx_copy().wait_recv()
+        gsum[...] = (g3[...] + g3x[...]).astype(BF16)
+        for d in range(1, NY):
+            gc_copy(d).start()
+        g4[y] = gsum[...]
 
     def g_chips():
-        for d, xx in peers:
-            s = (x if xx == 0 else 1 - x) * NY + yo(d)
-            copy(g3, g4.at[s], gc_s.at[xx * NY + d], gc_r.at[s], ctx=sib).wait_recv()
+        for d in range(1, NY):
+            copy(gsum, g4.at[yo(d)], gc_s.at[d], gc_r.at[yo(d)], ctx=sib).wait_recv()
         gfin[c] = jnp.sum(g4[...].astype(F32), axis=0)
         g4_copy().start()
 
@@ -489,11 +526,12 @@
         w = h * u
         ds = dw * (u + w * (1.0 - th))
         if diagonal:
-            ok = allowed()
+            lead = 64 * blocks
+            ok = allowed(lead, 128 * blocks)
 
             def masked(v):
-                first = jnp.where(ok, v[:256], 0.0)
-                return first if v.shape[0] == 256 else jnp.concatenate([first, v[256:]], axis=0)
+                first = jnp.where(ok, v[:lead], 0.0)
+                return first if v.shape[0] == lead else jnp.concatenate([first, v[lead:]], axis=0)
 
             w, ds = masked(w), masked(ds)
         w = w.astype(BF16)
@@ -577,6 +615,26 @@
     HALF = T // 2
     every = slice(0, 256 * T)
 
+    def own_step(t, tiles):
+        bwd(slice(256 * t, 256 * T), (x * T + t) * 4, 4 * tiles, True, False)
+
+        @pl.when(jnp.logical_or(x == 1, t >= HALF))
+        def _():
+            for i in range(2 * t, 2 * (t + tiles)):
+                sib_own(i).start()
+
+        @pl.when(x == 0)
+        def _():
+            for k in range(t, t + tiles):
+                send_dq(k, False)
+
+    if T == 2:
+        steps = [(0, 1), (1, 1)]
+    else:
+        steps = [(t, 1) for t in range(T - 2)] + [(T - 2, 2)]
+    own_step(*steps[0])
+
+
     @pl.when(x == 1)
     def _():
         for t in range(HALF, T):
@@ -585,25 +643,19 @@
                 sib_cross(2 * t + e).start()
             if t > HALF:
                 cross_sums(t - 1)
-
-    for t in range(T):
-        bwd(slice(256 * t, 256 * T), (x * T + t) * 4, 4, True, False)
-
-        @pl.when(jnp.logical_or(x == 1, t >= HALF))
-        def _():
-            for e in range(2):
-                sib_own(2 * t + e).start()
+            else:
+                send_dkv(0, False)
+
+    for n, (t, tiles) in list(enumerate(steps))[1:]:
+        own_step(t, tiles)
 
         @pl.when(x == 1)
         def _():
-            if t == 0:
+            if n == 1:
                 cross_sums(T - 1)
-            else:
-                send_dkv(t - 1, False)
-
-        @pl.when(x == 0)
-        def _():
-            send_dq(t, False)
+            for k in range(steps[n - 1][0], t):
+                if k:
+                    send_dkv(k, False)
 
     g_histories()
 
@@ -625,7 +677,8 @@
 
     @pl.when(x == 1)
     def _():
-        send_dkv(T - 1, False)
+        for k in range(steps[-1][0], T):
+            send_dkv(k, False)
 
     g_pair()
 
@@ -638,6 +691,8 @@
     def _():
         for t in list(range(HALF, T)) + list(range(HALF)):
             send_dkv(t, t >= HALF)
+
+    g_across()
 
     def finish_dq():
         for d in near_first:
@@ -692,8 +747,9 @@
     for d in range(1, NB):
         neg_copy(d).wait_send()
         gb_copy(d).wait_send()
-    for d, xx in peers:
-        gc_copy(d, xx).wait_send()
+    for d in range(1, NY):
+        gc_copy(d).wait_send()
+    gx_copy().wait_send()
     g1_copy().wait_send()
     g4_copy().wait_send()
 
@@ -745,7 +801,7 @@
                 V((8, D), BF16),
                 pltpu.SMEM((8,), I32),
                 pltpu.SMEM((8,), I32),
-                S((9,)),
+                S((12,)),
                 V((ROWS, 4 * D), F32),
                 V((NY, 128, 128), BF16),
                 V((NY, 64, 128), BF16),
@@ -781,15 +837,17 @@
                 V((NB, D // 16, 128), BF16),
                 V((D // 16, 128), F32),
                 V((D // 16, 128), F32),
+                V((D // 32, 128), F32),
+                V((D // 32, 128), F32),
                 V((D // 32, 128), BF16),
-                V((2 * NY, D // 32, 128), BF16),
+                V((NY, D // 32, 128), BF16),
                 V((2, D // 32, 128), F32),
             ]
             + [S((NY,))] * 32
             + [S((NB,))] * 4
             + [S((1,))] * 2
-            + [S((2 * NY,))] * 2
-            + [S((1,))] * 2
+            + [S((NY,))] * 2
+            + [S((1,))] * 4
             + [pltpu.SemaphoreType.REGULAR],
             compiler_params=pltpu.CompilerParams(
                 collective_id=0, has_side_effects=True, vmem_limit_bytes=60 << 20

time: 72.3 us -> 67.3 us (0.931)
  Pallas kernels: 67.4 us -> 62.4 us
    pallas_call x1, Pallas kernels: 67.4 us -> 62.4 us  [shards(): pl.pallas_call(body, out_shape=(jax.ShapeDtypeStruct((1, ROWS), F32), jax...]
where the time goes in v4:
time: 67.3 us; the launch traced here: 67.1 us
  Pallas kernels  62.4 us (93%)
  local copies, waits for them, and re-layouts  4.05 us (6%)
    pallas_call x1, Pallas kernels, shards(): pl.pallas_call(body, out_shape=(jax.ShapeDtypeStruct((1, ROWS), F32), jax...  62.4 us
    unnamed x3, local copies, waits for them, and re-layouts  4.05 us

profile of v4, /device:TPU:1, one launch (start us, length us, event | category | flops | bytes accessed | tf_op | source)
XLA Modules:
  0.0 67.1 jit_solution(12000146663582309392)
XLA Ops:
  0.6 62.4 %shard_map.103 = (f32[1,128]{1,0:T(1,128)}, bf16[1,128,512]{2,1,0:T(8,128)(2,1)}, f32[8,512]{1,0:T(8,128)}) custom-call(bf16[1,128,512]{2,1,0:T(8,128)(2,1)} %refs_0_.1, bf16[512,2048]{1,0:T(8,128)(2,1)} %refs_1_.1, bf16[512,512]{1,0:T(8,128)(2,1)} %refs_2_.1, bf16[1,128,512]{2,1,0:T(8,128)(2,1)} %refs_3_.1, s32[1,128]{1,0:T(1,128)} %refs_4_.1, ...), custom_call_target="tpu_custom_call" | custom-call | tf_op jit(solution)/shard_map/pallas_call | solution.py:786
  63.0 1.2 %copy.14 = f32[1,128]{1,0:T(1,128)} copy(f32[1,128]{1,0:T(1,128)} %get-tuple-element.6) | data formatting | bytes 1024
  64.2 1.6 %copy.15 = bf16[1,128,512]{2,1,0:T(8,128)(2,1)} copy(bf16[1,128,512]{2,1,0:T(8,128)(2,1)} %get-tuple-element.7) | data formatting | bytes 262144
  65.7 1.3 %copy.16 = f32[8,512]{1,0:T(8,128)} copy(f32[8,512]{1,0:T(8,128)} %get-tuple-element.8) | data formatting | bytes 32768

commit v5 on v4

--- a/solution.py
+++ b/solution.py
@@ -634,30 +634,46 @@
         steps = [(t, 1) for t in range(T - 2)] + [(T - 2, 2)]
     own_step(*steps[0])
 
-
-    @pl.when(x == 1)
-    def _():
-        for t in range(HALF, T):
-            bwd(every, 4 * t, 4, False, False)
-            for e in range(2):
-                sib_cross(2 * t + e).start()
-            if t > HALF:
-                cross_sums(t - 1)
-            else:
-                send_dkv(0, False)
-
-    for n, (t, tiles) in list(enumerate(steps))[1:]:
-        own_step(t, tiles)
-
-        @pl.when(x == 1)
-        def _():
-            if n == 1:
-                cross_sums(T - 1)
-            for k in range(steps[n - 1][0], t):
-                if k:
-                    send_dkv(k, False)
-
-    g_histories()
+    def cross_step(t):
+        bwd(every, 4 * t, 4, False, False)
+        for e in range(2):
+            sib_cross(2 * t + e).start()
+
+
+    @pl.when(x == 1)
+    def _():
+        cross_step(HALF)
+        send_dkv(0, False)
+        if T == 2:
+            cross_sums(HALF)
+
+    own_step(*steps[1])
+
+
+    @pl.when(x == 1)
+    def _():
+        if T > 2:
+            g_histories()
+            cross_sums(HALF)
+            cross_step(T - 1)
+            send_dkv(1, False)
+        else:
+            g_histories()
+        g_pair()
+
+    if T > 2:
+        own_step(*steps[2])
+
+
+    @pl.when(x == 1)
+    def _():
+        if T > 2:
+            cross_sums(T - 1)
+        g_across()
+
+    @pl.when(x == 0)
+    def _():
+        g_histories()
 
 
     @pl.when(x == 0)
@@ -671,6 +687,8 @@
                 i = n * T + e
                 sxq[i] = pack_dq(NY + i).astype(BF16)
                 dq_cross(i).start()
+            if n == 0:
+                g_pair()
         for i in range(2 * HALF):
             sib_own(i).start()
 
@@ -679,20 +697,18 @@
     def _():
         for k in range(steps[-1][0], T):
             send_dkv(k, False)
-
-    g_pair()
-
-    @pl.when(x == 1)
-    def _():
         for k in range(T):
             send_dq(k, True)
 
     @pl.when(x == 0)
     def _():
-        for t in list(range(HALF, T)) + list(range(HALF)):
-            send_dkv(t, t >= HALF)
-
-    g_across()
+        send_dkv(HALF, True)
+        g_across()
+        send_dkv(0, False)
+        for t in range(1, HALF):
+            send_dkv(t, False)
+        for t in range(HALF + 1, T):
+            send_dkv(t, True)
 
     def finish_dq():
         for d in near_first:
@@ -709,6 +725,7 @@
     def _():
         finish_dq()
 
+    g_chips()
     for d in near_first:
         yy = yo(d)
         copy(sret.at[yy], rret.at[yy], ret_s.at[yy], ret_r.at[yy], ctx=at(x, yy, c)).wait_recv()
@@ -719,7 +736,6 @@
         cols = slice(D + 128 * j, D + 128 * (j + 1))
         dpre[:, cols] = (jnp.where(lo, swap(even), odd) * slope(pre[:, cols])).astype(BF16)
     dout[...] += dot_nt(dpre[:, D : 2 * D], w_in_ref[:, D : 2 * D]) + dot_nt(dpre[:, 3 * D :], w_in_ref[:, 3 * D :])
-    g_chips()
 
     @pl.when(x == 1)
     def _():
@@ -786,9 +802,9 @@
         return pl.pallas_call(
             body,
             out_shape=(
-                jax.ShapeDtypeStruct((1, ROWS), F32),
-                jax.ShapeDtypeStruct((1, ROWS, D), BF16),
-                jax.ShapeDtypeStruct((8, D), F32),
+                V((1, ROWS), F32),
+                V((1, ROWS, D), BF16),
+                V((8, D), F32),
             ),
             in_specs=[pl.BlockSpec(memory_space=pltpu.HBM)] * 8,
             out_specs=(vm, vm, vm),

time: 67.3 us -> 64 us (0.951); the launches traced: 67.1 us -> 62.8 us
  local copies, waits for them, and re-layouts: 4.05 us -> 1.77 us
  Pallas kernels: 62.4 us -> 60.4 us
    unnamed x3, local copies, waits for them, and re-layouts: 4.05 us -> 1.77 us
    pallas_call x1, Pallas kernels: 62.4 us -> 60.4 us  [shards(): pl.pallas_call(body, out_shape=(V((1, ROWS), F32), V((1, ROWS, D), BF16),...]
where the time goes in v5:
time: 64 us; the launch traced here: 62.8 us
  Pallas kernels  60.4 us (94%)
  local copies, waits for them, and re-layouts  1.77 us (3%)
  between operations  0.64 us (1%)
    pallas_call x1, Pallas kernels, shards(): pl.pallas_call(body, out_shape=(V((1, ROWS), F32), V((1, ROWS, D), BF16),...  60.4 us
    unnamed x3, local copies, waits for them, and re-layouts  1.77 us

profile of v5, /device:TPU:1, one launch (start us, length us, event | category | flops | bytes accessed | tf_op | source)
XLA Modules:
  0.0 62.8 jit_solution(17102154793405805219)
XLA Ops:
  0.6 60.4 %shard_map.103 = (f32[1,128]{1,0:T(1,128)S(1)}, bf16[1,128,512]{2,1,0:T(8,128)(2,1)S(1)}, f32[8,512]{1,0:T(8,128)S(1)}) custom-call(bf16[1,128,512]{2,1,0:T(8,128)(2,1)} %refs_0_.1, bf16[512,2048]{1,0:T(8,128)(2,1)} %refs_1_.1, bf16[512,512]{1,0:T(8,128)(2,1)} %refs_2_.1, bf16[1,128,512]{2,1,0:T(8,128)(2,1)} %refs_3_.1, s32[1,128]{1,0:T(1,128)} %refs_4_.1, ...), custom_call_target="tpu_custom_call" | custom-call | tf_op jit(solution)/shard_map/pallas_call | solution.py:802
  61.0 0.5 copy.14
  61.6 0.6 copy.16
  62.2 0.7 %copy.15 = bf16[1,128,512]{2,1,0:T(8,128)(2,1)} copy(bf16[1,128,512]{2,1,0:T(8,128)(2,1)S(1)} %get-tuple-element.4) | data formatting | bytes 262144

commit v6 on v5

--- a/solution.py
+++ b/solution.py
@@ -94,17 +94,17 @@
                     (w_in_hbm.at[pl.ds(r * D // 4, D // 4), D:], w_in_ref.at[pl.ds(r * D // 4, D // 4), D:])
                     for r in range(4)
                 ],
-                (w_in_hbm.at[:, :D], w_in_ref.at[:, :D]),
                 (neg_hbm, neg_ref),
                 (nid_hbm, nid_ref),
                 (ncnt_hbm, ncnt_ref),
+                (w_in_hbm.at[:, :D], w_in_ref.at[:, :D]),
                 (pos_hbm, pos_ref),
                 (pid_hbm, pid_ref),
                 (w_out_hbm, w_out_ref),
             ]
         )
     ]
-    for load in loads:
+    for load in loads[:8]:
         load.start()
     barrier = pltpu.get_barrier_semaphore()
     for p in [sib, across] + others:
@@ -118,6 +118,8 @@
 
     for load in loads[:5]:
         load.wait()
+    for load in loads[8:]:
+        load.start()
     xin = seq_ref[0]
     lane = lax.broadcasted_iota(I32, (ROWS, 128), 1)
     lo = lane < HEAD
@@ -136,7 +138,7 @@
         sq[2 * j] = pack_rows(qt, 0).astype(BF16)
         sq[2 * j + 1] = pack_rows(qt, 1).astype(BF16)
 
-    for load in loads[5:]:
+    for load in loads[5:8]:
         load.wait()
     negs[:, :D] = neg_ref[...].astype(F32)
     meta_lane = lax.broadcasted_iota(I32, (8, 128), 1)
@@ -216,6 +218,8 @@
 
     nega[b] = negs[...]
 
+    for load in loads[8:]:
+        load.wait()
     g_pre = dot_nn(xin, w_in_ref[:, :D])
     pre[:, :D] = g_pre
 
@@ -368,9 +372,11 @@
         for n in range(2):
             piece = slice(W * n, W * (n + 1))
             acc[piece] += rows_of(qz[piece], tile, False)
-        for i in range(NY):
+        for d in far_first + [0]:
+            i = yo(d)
             mix_cross(i).wait_recv()
-            send_mixed(i, pack_mixed(acc[i * 128 : (i + 1) * 128], 0) + rmx[i].astype(F32))
+            rows = acc[pl.ds(pl.multiple_of(i * 128, 128), 128), :]
+            send_mixed(i, pack_mixed(rows, 0) + rmx[i].astype(F32))
 
     for d in range(1, NB):
         bb = bo(d)
@@ -571,12 +577,12 @@
         return copy(sret.at[i], rret.at[y], ret_s.at[i], ret_r.at[y], ctx=at(x, i, c))
 
     def pack_dq(i):
-        top = dq[i * 128 : i * 128 + 64] * 0.0625
-        bottom = dq[i * 128 + 64 : i * 128 + 128] * 0.0625
+        top = dq[pl.ds(pl.multiple_of(i * 128, 128), 64), :] * 0.0625
+        bottom = dq[pl.ds(pl.multiple_of(i * 128 + 64, 64), 64), :] * 0.0625
         return jnp.where(half, top, swap(bottom))
 
-    def send_dq(k, crossed):
-        for i in (2 * k, 2 * k + 1):
+    def send_dq(blocks, crossed):
+        for i in blocks:
             mine = pack_dq(i)
             if crossed:
                 dq_cross(i).wait_recv()
@@ -625,8 +631,7 @@
 
         @pl.when(x == 0)
         def _():
-            for k in range(t, t + tiles):
-                send_dq(k, False)
+            send_dq(range(2 * t, 2 * (t + tiles)), False)
 
     if T == 2:
         steps = [(0, 1), (1, 1)]
@@ -643,37 +648,32 @@
     @pl.when(x == 1)
     def _():
         cross_step(HALF)
+
+    own_step(*steps[1])
+
+
+    @pl.when(x == 1)
+    def _():
+        cross_sums(HALF)
         send_dkv(0, False)
-        if T == 2:
-            cross_sums(HALF)
-
-    own_step(*steps[1])
-
-
-    @pl.when(x == 1)
-    def _():
-        if T > 2:
-            g_histories()
-            cross_sums(HALF)
-            cross_step(T - 1)
-            send_dkv(1, False)
-        else:
-            g_histories()
-        g_pair()
 
     if T > 2:
         own_step(*steps[2])
 
-
-    @pl.when(x == 1)
-    def _():
+    g_histories()
+
+    @pl.when(x == 1)
+    def _():
+        send_dkv(1, False)
+        if T > 2:
+            cross_step(T - 1)
+        g_pair()
+        for k in range(2, T):
+            send_dkv(k, False)
         if T > 2:
             cross_sums(T - 1)
         g_across()
-
-    @pl.when(x == 0)
-    def _():
-        g_histories()
+        send_dq([yo(d) for d in far_first + [0]], True)
 
 
     @pl.when(x == 0)
@@ -692,13 +692,6 @@
         for i in range(2 * HALF):
             sib_own(i).start()
 
-
-    @pl.when(x == 1)
-    def _():
-        for k in range(steps[-1][0], T):
-            send_dkv(k, False)
-        for k in range(T):
-            send_dq(k, True)
 
     @pl.when(x == 0)
     def _():

time: 64 us -> 63.5 us (level)
  the two profiles are of different devices: /device:TPU:1 before, /device:TPU:192 now
where the time goes in v6:
time: 63.5 us; the launch traced here: 63.3 us
  Pallas kernels  60.9 us (96%)
  local copies, waits for them, and re-layouts  1.77 us (3%)
  between operations  0.64 us (1%)
    pallas_call x1, Pallas kernels, shards(): pl.pallas_call(body, out_shape=(V((1, ROWS), F32), V((1, ROWS, D), BF16),...  60.9 us
    unnamed x3, local copies, waits for them, and re-layouts  1.77 us

profile of v6, /device:TPU:192, one launch (start us, length us, event | category | flops | bytes accessed | tf_op | source)
XLA Modules:
  0.0 63.3 jit_solution(16017553352876801320)
XLA Ops:
  0.6 60.9 %shard_map.103 = (f32[1,128]{1,0:T(1,128)S(1)}, bf16[1,128,512]{2,1,0:T(8,128)(2,1)S(1)}, f32[8,512]{1,0:T(8,128)S(1)}) custom-call(bf16[1,128,512]{2,1,0:T(8,128)(2,1)} %refs_0_.1, bf16[512,2048]{1,0:T(8,128)(2,1)} %refs_1_.1, bf16[512,512]{1,0:T(8,128)(2,1)} %refs_2_.1, bf16[1,128,512]{2,1,0:T(8,128)(2,1)} %refs_3_.1, s32[1,128]{1,0:T(1,128)} %refs_4_.1, ...), custom_call_target="tpu_custom_call" | custom-call | tf_op jit(solution)/shard_map/pallas_call | solution.py:795
  61.6 0.5 copy.14
  62.1 0.6 copy.16
  62.7 0.7 %copy.15 = bf16[1,128,512]{2,1,0:T(8,128)(2,1)} copy(bf16[1,128,512]{2,1,0:T(8,128)(2,1)S(1)} %get-tuple-element.4) | data formatting | bytes 262144

commit v7 on v6

--- a/solution.py
+++ b/solution.py
@@ -285,19 +285,21 @@
     def _():
         meet_higher()
 
-    for d in range(NY):
-        yy = yo(d)
-        r = at(x, yy, 1 - c)
-        copy(kv.at[r], kv.at[r], rel_s.at[yy], rel_r.at[yy], ctx=sib).wait_recv()
+    def relay_in(i):
+        r = at(x, i, 1 - c)
+        return copy(kv.at[r], kv.at[r], rel_s.at[i], rel_r.at[i], ctx=sib)
+
+    for i in range(E):
+        relay_in(i).wait_recv()
 
 
     @pl.when(x == 0)
     def _():
-        for i in range(NY):
-            q_forward(i).wait_recv()
-            take_q(NY + i)
         tile = kv[:NY].reshape(128 * NY, 128)
         for n in range(2):
+            for i in range(n * T, (n + 1) * T):
+                q_forward(i).wait_recv()
+                take_q(NY + i)
             w = weighted(qz[256 * T + W * n : 256 * T + W * (n + 1)], tile)
             rows = dot_nn(w.astype(BF16), tile)
             for e in range(T):
@@ -305,6 +307,9 @@
                 mix_cross(n * T + e).start()
         meet_higher()
         take_own_q()
+
+    for i in range(E, NY):
+        relay_in(i).wait_recv()
 
     def keys_of(t):
         return kv[pl.ds(t * 4, 4)].reshape(512, 128)

time: 63.5 us -> 63.4 us (level)
  the two profiles are of different devices: /device:TPU:192 before, /device:TPU:1 now
where the time goes in v7:
time: 63.4 us; the launch traced here: 62.3 us
  Pallas kernels  59.9 us (94%)
  local copies, waits for them, and re-layouts  1.77 us (3%)
  between operations  0.64 us (1%)
    pallas_call x1, Pallas kernels, shards(): pl.pallas_call(body, out_shape=(V((1, ROWS), F32), V((1, ROWS, D), BF16),...  59.9 us
    unnamed x3, local copies, waits for them, and re-layouts  1.77 us

profile of v7, /device:TPU:1, one launch (start us, length us, event | category | flops | bytes accessed | tf_op | source)
XLA Modules:
  0.0 62.3 jit_solution(8298696881823014991)
XLA Ops:
  0.6 59.9 %shard_map.103 = (f32[1,128]{1,0:T(1,128)S(1)}, bf16[1,128,512]{2,1,0:T(8,128)(2,1)S(1)}, f32[8,512]{1,0:T(8,128)S(1)}) custom-call(bf16[1,128,512]{2,1,0:T(8,128)(2,1)} %refs_0_.1, bf16[512,2048]{1,0:T(8,128)(2,1)} %refs_1_.1, bf16[512,512]{1,0:T(8,128)(2,1)} %refs_2_.1, bf16[1,128,512]{2,1,0:T(8,128)(2,1)} %refs_3_.1, s32[1,128]{1,0:T(1,128)} %refs_4_.1, ...), custom_call_target="tpu_custom_call" | custom-call | tf_op jit(solution)/shard_map/pallas_call | solution.py:800
  60.5 0.5 copy.14
  61.1 0.6 copy.16
  61.7 0.7 %copy.15 = bf16[1,128,512]{2,1,0:T(8,128)(2,1)} copy(bf16[1,128,512]{2,1,0:T(8,128)(2,1)S(1)} %get-tuple-element.4) | data formatting | bytes 262144
